TPU v7x, 128 devices: a whole 4x4x4 slice. The times are simulated.
128 devices in a mesh: gx: 8 (over x, core), yz: 16 (over y, z).
Axes of the slice: x: 4, y: 4, z: 4, core: 2. Of those that a mesh axis runs over, the one named last changes fastest.
Arguments:
- right_side: float32 [3, 64, 2048, 256], P(None, 'gx', 'yz'), may hold values from -30 to 30
- viscosity: bfloat16 [64, 2048, 256], P('gx', 'yz'), may hold values from 0.29882812 to 3
- strain_rate: bfloat16 [6, 64, 2048, 256], P(None, 'gx', 'yz'), may hold values from -6 to 6
- cell_code: int32 [64, 2048, 256], P('gx', 'yz'), may hold values from 0 to 2
Outputs:
- solution_field: float32 [3, 64, 2048, 256], P(None, 'gx', 'yz')
- residual: float32 [3, 64, 2048, 256], P(None, 'gx', 'yz')
All inputs are finite; a program needn't handle non-finite values.
Results may differ from a plain program's by a relative error of at most 0.0003.
Values may be sent and summed in bfloat16 or wider, within the bound.
No kernel may reach another device: no remote copies, remote signals or barrier semaphores. Data moves between devices by JAX's collectives and lax.ppermute only.
A program may use at most 128 MiB of HBM per device.

v0:
```python
import jax
import jax.numpy as jnp
from jax import lax
from jax.sharding import PartitionSpec as P

ITERS = 3


SOFTEN = 0.8


def from_behind(x, axis, by):
    peers = lax.axis_size(axis)
    pairs = [(i, i + by) for i in range(peers) if 0 <= i + by < peers]
    return lax.ppermute(x, axis, pairs)


def stresses(base, next_x, next_y, next_z, viscosity, strain_rate):
    along_x = next_x - base
    along_y = next_y - base
    along_z = next_z - base
    strain = strain_rate.astype(jnp.float32)
    two_eta = 2.0 * viscosity.astype(jnp.float32)
    parts = [
        along_x[0],
        along_y[1],
        along_z[2],
        0.5 * (along_y[0] + along_x[1]),
        0.5 * (along_z[0] + along_x[2]),
        0.5 * (along_z[1] + along_y[2]),
    ]
    self_dot = (
        strain[0] * strain[0]
        + strain[1] * strain[1]
        + strain[2] * strain[2]
        + 2.0 * (strain[3] * strain[3] + strain[4] * strain[4] + strain[5] * strain[5])
    )
    cross_dot = (
        strain[0] * parts[0]
        + strain[1] * parts[1]
        + strain[2] * parts[2]
        + 2.0 * (strain[3] * parts[3] + strain[4] * parts[4] + strain[5] * parts[5])
    )
    factor = SOFTEN * cross_dot / (1.0 + self_dot)
    taus = [two_eta * (parts[k] - factor * strain[k]) for k in range(6)]
    flux_x = jnp.stack([taus[0], taus[3], taus[4]])
    flux_y = jnp.stack([taus[3], taus[1], taus[5]])
    flux_z = jnp.stack([taus[4], taus[5], taus[2]])
    return (flux_x, flux_y, flux_z)


def divergence(own_x, prev_x, own_y, prev_y, own_z, prev_z):
    return prev_x - own_x + (prev_y - own_y) + (prev_z - own_z)


def operate_shifts(field, viscosity, strain_rate, mask, weight):
    masked = mask * field
    zero_z = jnp.zeros_like(masked[..., :1])
    face_x = from_behind(masked[:, :1], "gx", -1)
    face_y = from_behind(masked[:, :, :1], "yz", -1)
    next_x = jnp.concatenate([masked[:, 1:], face_x], 1)
    next_y = jnp.concatenate([masked[:, :, 1:], face_y], 2)
    next_z = jnp.concatenate([masked[..., 1:], zero_z], 3)
    flux_x, flux_y, flux_z = stresses(masked, next_x, next_y, next_z, viscosity, strain_rate)
    lower_x = from_behind(flux_x[:, -1:], "gx", 1)
    lower_y = from_behind(flux_y[:, :, -1:], "yz", 1)
    prev_x = jnp.concatenate([lower_x, flux_x[:, :-1]], 1)
    prev_y = jnp.concatenate([lower_y, flux_y[:, :, :-1]], 2)
    prev_z = jnp.concatenate([zero_z, flux_z[..., :-1]], 3)
    return mask * divergence(flux_x, prev_x, flux_y, prev_y, flux_z, prev_z) + weight * field


def per_device(right_side, viscosity, strain_rate, cell_code):
    mask = (cell_code != 0).astype(jnp.float32)
    weight = jnp.where(cell_code == 0, 1.0, jnp.where(cell_code == 1, 0.2, 1.2)).astype(jnp.float32)
    solution_field = jnp.zeros_like(right_side)
    residual = right_side

    def squares(vector):
        return lax.psum(jnp.sum(vector * vector), ("gx", "yz"))

    direction = right_side
    norm_now = squares(residual)
    for iteration in range(ITERS):
        image = operate_shifts(direction, viscosity, strain_rate, mask, weight)
        alpha = norm_now / lax.psum(jnp.sum(direction * image), ("gx", "yz"))
        solution_field = solution_field + alpha * direction
        residual = residual - alpha * image
        norm_next = squares(residual)
        direction = residual + norm_next / norm_now * direction
        norm_now = norm_next
    return (solution_field, residual)


def solution(mesh):
    placed = (
        P(None, "gx", "yz", None),
        P("gx", "yz", None),
        P(None, "gx", "yz", None),
        P("gx", "yz", None),
    )
    return jax.shard_map(
        per_device,
        mesh=mesh,
        in_specs=placed,
        out_specs=(P(None, "gx", "yz", None), P(None, "gx", "yz", None)),
        check_vma=False,
    )
```

profile of v0, /device:TPU:1, one launch (start us, length us, event | category | flops | bytes accessed | tf_op | source)
XLA Modules:
  0.0 452.5 jit_solution(16307602607647411352)
XLA Ops:
  2.0 2.6 broadcast_multiply_fusion.2
  4.6 3.3 collective-permute-start
  23.1 3.1 collective-permute-start.2
  26.3 4.3 collective-permute-start.3
  31.5 4.4 multiply_reduce_fusion.4
  35.9 71.1 %all-reduce.6 = (f32[]{:T(128)}, f32[]{:T(128)}) all-reduce(f32[]{:T(128)} %get-tuple-element.3, f32[]{:T(128)} %get-tuple-element.2), channel_id=1, replica_groups=mesh['gx'=8,'yz'=16] {'gx','yz'}, use_global_device_ids=true, to_apply=%region_1.2 | all-reduce | flops 2 | bytes 16 | tf_op jit(solution)/shard_map/psum | solution.py:80
  108.4 3.3 multiply_reduce_fusion.3
  111.7 63.1 %psum.44 = f32[]{:T(128)} all-reduce(f32[]{:T(128)} %multiply_reduce_fusion.3), channel_id=1, replica_groups=mesh['gx'=8,'yz'=16] {'gx','yz'}, use_global_device_ids=true, to_apply=%region_5.6 | all-reduce | flops 1 | bytes 8 | tf_op jit(solution)/shard_map/psum | solution.py:80
  176.2 2.9 broadcast_multiply_fusion.1
  179.1 2.6 collective-permute-start.4
  188.2 3.1 maximum_subtract_fusion.4
  195.5 2.7 collective-permute-start.6
  198.3 2.9 collective-permute-start.7
  202.9 4.5 multiply_reduce_fusion.2
  207.4 66.4 %psum.45 = f32[]{:T(128)} all-reduce(f32[]{:T(128)} %get-tuple-element.14), channel_id=1, replica_groups=mesh['gx'=8,'yz'=16] {'gx','yz'}, use_global_device_ids=true, to_apply=%region_7.8 | all-reduce | flops 1 | bytes 8 | tf_op jit(solution)/shard_map/psum | solution.py:86
  275.1 6.1 %multiply_reduce_fusion.1 = (f32[]{:T(128)}, f32[3,8,128,256]{3,2,1,0:T(8,128)}) fusion(f32[3,8,128,256]{3,2,1,0:T(8,128)} %get-tuple-element.15, f32[]{:T(128)S(6)} %div.28, f32[3,8,128,256]{3,2,1,0:T(8,128)S(1)} %copy-done.1, f32[3,8,128,256]{3,2,1,0:T(8,128)} %get-tuple-element.20, f32[]{:T(128)S(6)} %div.25), kind=kLoop, calls=%fused_computation.38 | loop fusion | flops 4718591 | bytes 12582924 | tf_op jit(solution)/shard_map/reduce_sum | solution.py:80
  281.1 62.5 %psum.46 = f32[]{:T(128)} all-reduce(f32[]{:T(128)} %get-tuple-element.12), channel_id=1, replica_groups=mesh['gx'=8,'yz'=16] {'gx','yz'}, use_global_device_ids=true, to_apply=%region_9.10 | all-reduce | flops 1 | bytes 8 | tf_op jit(solution)/shard_map/psum | solution.py:80
  344.9 3.8 broadcast_multiply_fusion
  348.7 2.4 collective-permute-start.8
  364.5 2.4 collective-permute-start.10
  366.9 2.6 collective-permute-start.11
  371.6 4.2 multiply_reduce_fusion
  375.7 66.1 %psum.47 = f32[]{:T(128)} all-reduce(f32[]{:T(128)} %get-tuple-element.6), channel_id=1, replica_groups=mesh['gx'=8,'yz'=16] {'gx','yz'}, use_global_device_ids=true, to_apply=%region_11.12 | all-reduce | flops 1 | bytes 8 | tf_op jit(solution)/shard_map/psum | solution.py:86
  443.0 9.5 %multiply_subtract_fusion = (f32[3,8,128,256]{3,2,1,0:T(8,128)}, f32[3,8,128,256]{3,2,1,0:T(8,128)}) fusion(f32[3,8,128,256]{3,2,1,0:T(8,128)} %get-tuple-element.13, f32[3,8,128,256]{3,2,1,0:T(8,128)} %get-tuple-element.7, f32[]{:T(128)S(6)} %div.31, f32[3,8,128,256]{3,2,1,0:T(8,128)} %copy-done.7, f32[3,8,128,256]{3,2,1,0:T(8,128)} %copy-done.6, ...), kind=kLoop, calls=%fused_computation.33 | loop fusion | flops 5505024 | bytes 22020108 | tf_op jit(solution)/shard_map/sub | solution.py:88
  (96 shorter events, 45.0 us)
Async XLA Ops:
  2.0 29.5 %copy-start.2 = (f32[8,128,256]{2,1,0:T(8,128)}, f32[8,128,256]{2,1,0:T(8,128)S(1)}, u32[]{:S(2)}) copy-start(f32[8,128,256]{2,1,0:T(8,128)S(1)} %compare_convert_fusion) | copy-start | bytes 3145732
  4.6 10.0 %collective-permute-start = (f32[3,1,128,256]{3,2,1,0:T(8,128)S(1)}, f32[3,1,128,256]{3,2,1,0:T(8,128)S(1)}, u32[]{:S(2)}, u32[]{:S(2)}) collective-permute-start(f32[3,1,128,256]{3,2,1,0:T(8,128)S(1)} %slice.319), channel_id=1, source_target_pairs={{16,0},{32,16},{48,32},{64,48},{80,64},{96,80},{112,96},{17,1},{33... | collective-permute-start | bytes 1179656 | tf_op jit(solution)/shard_map/ppermute | solution.py:15
  8.0 4.9 %collective-permute-start.1 = (f32[3,8,1,256]{3,2,1,0:T(1,128)S(1)}, f32[3,8,1,256]{3,2,1,0:T(1,128)S(1)}, u32[]{:S(2)}, u32[]{:S(2)}) collective-permute-start(f32[3,8,1,256]{3,2,1,0:T(1,128)S(1)} %slice.324), channel_id=1, source_target_pairs={{1,0},{2,1},{3,2},{4,3},{5,4},{6,5},{7,6},{8,7},{9,8},{10,9},{11,1... | collective-permute-start | bytes 73736 | tf_op jit(solution)/shard_map/ppermute | solution.py:15
  12.3 8.0 %copy-start = (f32[6,8,128,256]{3,2,1,0:T(8,128)}, f32[6,8,128,256]{3,2,1,0:T(8,128)S(1)}, u32[]{:S(2)}) copy-start(f32[6,8,128,256]{3,2,1,0:T(8,128)S(1)} %convert_element_type.15) | copy-start | bytes 18874372
  12.3 6.2 %copy-start.8 = (bf16[8,128,256]{2,1,0:T(8,128)(2,1)S(1)}, bf16[8,128,256]{2,1,0:T(8,128)(2,1)}, u32[]{:S(2)}) copy-start(bf16[8,128,256]{2,1,0:T(8,128)(2,1)} %param.5) | copy-start | bytes 1572868
  21.8 8.7 %copy-start.14 = (s32[8,128,256]{2,1,0:T(8,128)S(1)}, s32[8,128,256]{2,1,0:T(8,128)}, u32[]{:S(2)}) copy-start(s32[8,128,256]{2,1,0:T(8,128)} %param.7) | copy-start | bytes 3145732
  23.1 8.4 %collective-permute-start.2 = (f32[3,1,128,256]{3,2,1,0:T(8,128)S(1)}, f32[3,1,128,256]{3,2,1,0:T(8,128)S(1)}, u32[]{:S(2)}, u32[]{:S(2)}) collective-permute-start(f32[3,1,128,256]{3,2,1,0:T(8,128)S(1)} %slice.338), channel_id=1, source_target_pairs={{0,16},{16,32},{32,48},{48,64},{64,80},{80,96},{96,112},{1,17},{17... | collective-permute-start | bytes 1179656 | tf_op jit(solution)/shard_map/ppermute | solution.py:15
  26.3 5.2 %collective-permute-start.3 = (f32[3,8,1,256]{3,2,1,0:T(1,128)S(1)}, f32[3,8,1,256]{3,2,1,0:T(1,128)S(1)}, u32[]{:S(2)}, u32[]{:S(2)}) collective-permute-start(f32[3,8,1,256]{3,2,1,0:T(1,128)S(1)} %slice.340), channel_id=1, source_target_pairs={{0,1},{1,2},{2,3},{3,4},{4,5},{5,6},{6,7},{7,8},{8,9},{9,10},{10,1... | collective-permute-start | bytes 73736 | tf_op jit(solution)/shard_map/ppermute | solution.py:15
  179.1 23.8 %copy-start.6 = (f32[3,8,128,256]{3,2,1,0:T(8,128)}, f32[3,8,128,256]{3,2,1,0:T(8,128)S(1)}, u32[]{:S(2)}) copy-start(f32[3,8,128,256]{3,2,1,0:T(8,128)S(1)} %get-tuple-element.19) | copy-start | bytes 9437188
  179.1 9.1 %collective-permute-start.4 = (f32[3,1,128,256]{3,2,1,0:T(8,128)S(1)}, f32[3,1,128,256]{3,2,1,0:T(8,128)S(1)}, u32[]{:S(2)}, u32[]{:S(2)}) collective-permute-start(f32[3,1,128,256]{3,2,1,0:T(8,128)S(1)} %slice.344), channel_id=1, source_target_pairs={{16,0},{32,16},{48,32},{64,48},{80,64},{96,80},{112,96},{17,1},{33... | collective-permute-start | bytes 1179656 | tf_op jit(solution)/shard_map/ppermute | solution.py:15
  181.7 4.8 %collective-permute-start.5 = (f32[3,8,1,256]{3,2,1,0:T(1,128)S(1)}, f32[3,8,1,256]{3,2,1,0:T(1,128)S(1)}, u32[]{:S(2)}, u32[]{:S(2)}) collective-permute-start(f32[3,8,1,256]{3,2,1,0:T(1,128)S(1)} %slice.347), channel_id=1, source_target_pairs={{1,0},{2,1},{3,2},{4,3},{5,4},{6,5},{7,6},{8,7},{9,8},{10,9},{11,1... | collective-permute-start | bytes 73736 | tf_op jit(solution)/shard_map/ppermute | solution.py:15
  195.4 7.5 %copy-start.3 = (f32[8,128,256]{2,1,0:T(8,128)S(1)}, f32[8,128,256]{2,1,0:T(8,128)}, u32[]{:S(2)}) copy-start(f32[8,128,256]{2,1,0:T(8,128)} %copy-done.2) | copy-start | bytes 3145732
  195.4 7.5 %copy-start.12 = (f32[8,128,256]{2,1,0:T(8,128)S(1)}, f32[8,128,256]{2,1,0:T(8,128)}, u32[]{:S(2)}) copy-start(f32[8,128,256]{2,1,0:T(8,128)} %copy-done.11) | copy-start | bytes 3145732
  195.5 7.4 %collective-permute-start.6 = (f32[3,1,128,256]{3,2,1,0:T(8,128)S(1)}, f32[3,1,128,256]{3,2,1,0:T(8,128)S(1)}, u32[]{:S(2)}, u32[]{:S(2)}) collective-permute-start(f32[3,1,128,256]{3,2,1,0:T(8,128)S(1)} %slice.357), channel_id=1, source_target_pairs={{0,16},{16,32},{32,48},{48,64},{64,80},{80,96},{96,112},{1,17},{17... | collective-permute-start | bytes 1179656 | tf_op jit(solution)/shard_map/ppermute | solution.py:15
  198.3 3.9 collective-permute-start.7
  348.7 22.9 %copy-start.7 = (f32[3,8,128,256]{3,2,1,0:T(8,128)}, f32[3,8,128,256]{3,2,1,0:T(8,128)S(1)}, u32[]{:S(2)}) copy-start(f32[3,8,128,256]{3,2,1,0:T(8,128)S(1)} %get-tuple-element.11) | copy-start | bytes 9437188
  348.7 9.3 %collective-permute-start.8 = (f32[3,1,128,256]{3,2,1,0:T(8,128)S(1)}, f32[3,1,128,256]{3,2,1,0:T(8,128)S(1)}, u32[]{:S(2)}, u32[]{:S(2)}) collective-permute-start(f32[3,1,128,256]{3,2,1,0:T(8,128)S(1)} %slice.363), channel_id=1, source_target_pairs={{16,0},{32,16},{48,32},{64,48},{80,64},{96,80},{112,96},{17,1},{33... | collective-permute-start | bytes 1179656 | tf_op jit(solution)/shard_map/ppermute | solution.py:15
  351.2 4.7 %collective-permute-start.9 = (f32[3,8,1,256]{3,2,1,0:T(1,128)S(1)}, f32[3,8,1,256]{3,2,1,0:T(1,128)S(1)}, u32[]{:S(2)}, u32[]{:S(2)}) collective-permute-start(f32[3,8,1,256]{3,2,1,0:T(1,128)S(1)} %slice.366), channel_id=1, source_target_pairs={{1,0},{2,1},{3,2},{4,3},{5,4},{6,5},{7,6},{8,7},{9,8},{10,9},{11,1... | collective-permute-start | bytes 73736 | tf_op jit(solution)/shard_map/ppermute | solution.py:15
  353.9 6.4 %slice-start.2 = ((s8[6291456]{0:T(1024)(128)(4,1)}), s8[4194304]{0:T(1024)(128)(4,1)S(1)}, s32[]{:S(2)}) async-start(s8[6291456]{0:T(1024)(128)(4,1)} %bitcast.272), calls=%async_computation.2 | async-start | bytes 8388608
  354.2 6.1 %slice-start.3 = ((s8[6291456]{0:T(1024)(128)(4,1)}), s8[2097152]{0:T(1024)(128)(4,1)S(1)}, s32[]{:S(2)}) async-start(s8[6291456]{0:T(1024)(128)(4,1)} %bitcast.272), calls=%async_computation.3 | async-start | bytes 4194304
  364.4 7.1 %copy-start.4 = (f32[8,128,256]{2,1,0:T(8,128)S(1)}, f32[8,128,256]{2,1,0:T(8,128)}, u32[]{:S(2)}) copy-start(f32[8,128,256]{2,1,0:T(8,128)} %copy-done.2) | copy-start | bytes 3145732
  364.5 7.1 %copy-start.13 = (f32[8,128,256]{2,1,0:T(8,128)S(1)}, f32[8,128,256]{2,1,0:T(8,128)}, u32[]{:S(2)}) copy-start(f32[8,128,256]{2,1,0:T(8,128)} %copy-done.11) | copy-start | bytes 3145732
  364.5 7.1 %collective-permute-start.10 = (f32[3,1,128,256]{3,2,1,0:T(8,128)S(1)}, f32[3,1,128,256]{3,2,1,0:T(8,128)S(1)}, u32[]{:S(2)}, u32[]{:S(2)}) collective-permute-start(f32[3,1,128,256]{3,2,1,0:T(8,128)S(1)} %slice.376), channel_id=1, source_target_pairs={{0,16},{16,32},{32,48},{48,64},{64,80},{80,96},{96,112},{1,17},{17... | collective-permute-start | bytes 1179656 | tf_op jit(solution)/shard_map/ppermute | solution.py:15
  366.9 3.5 collective-permute-start.11
  (9 other events, 42.4 us)
where the time goes:
time: 454 us; the launch traced here: 453 us
  blocking collectives  329 us (72%)
  other arithmetic  63.6 us (14%)
  starting transfers between devices  30.5 us (7%)
  waiting for transfers between devices  12.1 us (3%)
  local copies, waits for them, and re-layouts  9.37 us (2%)
  between operations  7.67 us (2%)
    psum x3, blocking collectives, squares(): return lax.psum(jnp.sum(vector * vector), ('gx', 'yz'))  197 us
    psum x2, blocking collectives, per_device(): alpha = norm_now / lax.psum(jnp.sum(direction * image), ('gx', 'yz'))  133 us
    ppermute x12, starting transfers between devices, from_behind(): return lax.ppermute(x, axis, pairs)  30.5 us
    reduce_sum x3, other arithmetic, per_device(): alpha = norm_now / lax.psum(jnp.sum(direction * image), ('gx', 'yz'))  13.1 us
    ppermute x12, waiting for transfers between devices, from_behind(): return lax.ppermute(x, axis, pairs)  12.1 us
    sub x1, other arithmetic, per_device(): residual = residual - alpha * image  9.53 us
    reduce_sum x2, other arithmetic, squares(): return lax.psum(jnp.sum(vector * vector), ('gx', 'yz'))  9.37 us
    mul x3, other arithmetic, operate_shifts(): masked = mask * field  9.22 us
  transfers between devices with their start and end apart: 12, of which 11 were waited for; matrix products, arithmetic and copies ran while one was open for 2% of the time, Pallas kernels for 0%

commit v1 on v0

v1 whole, which is shorter than its diff:
```python
import jax
import jax.numpy as jnp
from jax import lax
from jax.experimental import pallas as pl
from jax.experimental.pallas import tpu as pltpu
from jax.sharding import PartitionSpec as P

SOFTEN = 0.8
F32 = jnp.float32
BF16 = jnp.bfloat16
LANES = 128
ROWS = 8
VMEM = pltpu.VMEM


def resident(shape, dtype=F32):
    return VMEM(shape, dtype)


def in_vmem(x):
    return pltpu.with_memory_space_constraint(x, VMEM)


def call(kernel, name, ins, outs, scratch=(), aliases=None, limit=24, cost=(1e6, 1e6)):
    specs, args = [], []
    for kind, x in ins:
        if kind == "hbm":
            specs.append(pl.BlockSpec(memory_space=pl.ANY))
            args.append(x)
        elif kind == "smem":
            specs.append(pl.BlockSpec(memory_space=pltpu.SMEM))
            args.append(x)
        else:
            specs.append(pl.BlockSpec(memory_space=VMEM))
            args.append(in_vmem(x))
    out_specs = [
        pl.BlockSpec(memory_space=VMEM) if isinstance(o, type(VMEM((8, 128), F32))) else pl.BlockSpec(memory_space=pl.ANY)
        for o in outs
    ]
    return pl.pallas_call(
        kernel,
        name=name,
        out_shape=outs,
        in_specs=specs,
        out_specs=out_specs,
        scratch_shapes=list(scratch),
        input_output_aliases=aliases or {},
        compiler_params=pltpu.CompilerParams(vmem_limit_bytes=limit << 20),
        cost_estimate=pl.CostEstimate(flops=int(cost[0]), bytes_accessed=int(cost[1]), transcendentals=0),
    )(*args)


def iotas():
    row = lax.broadcasted_iota(jnp.int32, (ROWS, LANES), 0)
    lane = lax.broadcasted_iota(jnp.int32, (ROWS, LANES), 1)
    return row, lane


def at(t, h):
    return pl.ds(ROWS * t, ROWS), pl.ds(LANES * h, LANES)


def weight_of(code):
    return jnp.where(code == 0, 0.0, jnp.where(code == 1, 0.2, 1.2)).astype(F32)


def tensor_of(visc, strain):
    two_eta = 2.0 * visc
    square = (
        strain[0] * strain[0]
        + strain[1] * strain[1]
        + strain[2] * strain[2]
        + 2.0 * (strain[3] * strain[3] + strain[4] * strain[4] + strain[5] * strain[5])
    )
    scale = jnp.sqrt(SOFTEN * two_eta / (1.0 + square))
    return [two_eta] + [scale * s for s in strain]


def split(x):
    high = x.astype(BF16)
    return high, (x - high.astype(F32)).astype(BF16)


def pack_kernel(par, b, visc, strain, code, ya, yb, xa, xb, tb, tv, ts, tc, lb, lc, sem):
    nl, nrow = b.shape[1], b.shape[2]
    copies = []
    for i, r in enumerate((0, nrow - ROWS)):
        rows = pl.ds(r, ROWS)
        copies.append(pltpu.make_async_copy(b.at[:, :, rows, :], tb.at[i], sem.at[i, 0]))
        copies.append(pltpu.make_async_copy(visc.at[:, rows, :], tv.at[i], sem.at[i, 1]))
        copies.append(pltpu.make_async_copy(strain.at[:, :, rows, :], ts.at[i], sem.at[i, 2]))
        copies.append(pltpu.make_async_copy(code.at[:, rows, :], tc.at[i], sem.at[i, 3]))
    px = par[0]
    py = par[1]
    late = []
    for i, out in enumerate((xa, xb)):
        layer = jnp.where(px == i, nl - 1, 0)
        copies.append(pltpu.make_async_copy(b.at[:, layer], lb.at[i], sem.at[i, 4]))
        copies.append(pltpu.make_async_copy(code.at[layer], lc.at[i], sem.at[i, 5]))
        late.append(pltpu.make_async_copy(visc.at[layer], out.at[6], sem.at[i, 6]))
        late.append(pltpu.make_async_copy(strain.at[:, layer], out.at[pl.ds(7, 6)], sem.at[i, 7]))
    for c in copies + late:
        c.start()
    for c in copies:
        c.wait()
    for i, out in enumerate((ya, yb)):
        slot = jnp.where(py == i, 1, 0)
        for l in range(nl):
            held = tc[slot, l] == 0
            for k in range(3):
                high, low = split(jnp.where(held, 0.0, tb[slot, k, l]))
                out[k, l] = high
                out[3 + k, l] = low
            out[6, l] = tv[slot, l]
            for k in range(6):
                out[7 + k, l] = ts[slot, k, l]
            out[13, l] = tc[slot, l].astype(F32).astype(BF16)
    for i, out in enumerate((xa, xb)):
        for t in range(nrow // 16):
            rows = pl.ds(16 * t, 16)
            held = lc[i, rows, :] == 0
            for k in range(3):
                high, low = split(jnp.where(held, 0.0, lb[i, k, rows, :]))
                out[k, rows, :] = high
                out[3 + k, rows, :] = low
    for c in late:
        c.wait()


def load_kernel(b, visc, strain, code, raw, es, m0, w, acc, sv, ss, sc, sem):
    nl, nrow = b.shape[1], b.shape[2]
    copies = []
    for l in range(nl):
        copies.append(
            [
                pltpu.make_async_copy(b.at[:, l], raw.at[:, l], sem.at[l, 0]),
                pltpu.make_async_copy(visc.at[l], sv.at[l], sem.at[l, 1]),
                pltpu.make_async_copy(strain.at[:, l], ss.at[l], sem.at[l, 2]),
                pltpu.make_async_copy(code.at[l], sc.at[l], sem.at[l, 3]),
            ]
        )
        for c in copies[-1]:
            c.start()
    zero = jnp.zeros((ROWS, LANES), F32)

    def chunk(l, u, carry):
        sums, helds = carry
        base = pl.multiple_of(16 * u, 16)
        rows16 = pl.ds(base, 16)
        v16 = sv[l, rows16, :].astype(F32)
        s16 = [ss[l, k, rows16, :].astype(F32) for k in range(6)]
        for i in range(2):
            for h in range(2):
                cut = lambda x: x[ROWS * i : ROWS * (i + 1), LANES * h : LANES * (h + 1)]
                rows, cols = pl.ds(pl.multiple_of(base + ROWS * i, ROWS), ROWS), pl.ds(LANES * h, LANES)
                weight = weight_of(sc[l, rows, cols])
                w[l, rows, cols] = weight
                for k, value in enumerate(tensor_of(cut(v16), [cut(s) for s in s16])):
                    es[l, k, rows, cols] = value
                for k in range(3):
                    x = raw[k, l, rows, cols]
                    m = jnp.where(weight > 0.0, x, 0.0)
                    m0[k, l, rows, cols] = m
                    rest = x - m
                    sums = sums + m * m
                    helds = helds + rest * rest
        return sums, helds

    carry = (zero, zero)
    for l in range(nl):
        for c in copies[l]:
            c.wait()
        carry = lax.fori_loop(0, nrow // 16, lambda u, s: chunk(l, u, s), carry)
    acc[0] = carry[0]
    acc[1] = carry[1]


def halo_kernel(par, ra, rb, es_in, m0_in, w_in, es, m0, w, ca, cb):
    row, _ = iotas()
    row2 = lax.broadcasted_iota(jnp.int32, (ROWS, 2 * LANES), 0)
    nl = ra.shape[1]
    halo = es.shape[2] - ROWS
    px = par[0]
    py = par[1]
    rows = pl.ds(halo, ROWS)

    def pick(k, l):
        a, c = ra[k, l].astype(F32), rb[k, l].astype(F32)
        even = (py == 0).astype(jnp.int32) + jnp.zeros_like(row2)
        upper = jnp.where(even == 1, a, c)
        lower = jnp.where(even == 1, c, a)
        return jnp.where(row2 < 3, upper, jnp.where(row2 >= 5, lower, 0.0))

    def layer(l, _):
        got = [pick(k, l) for k in range(14)]
        w[l, rows, :] = weight_of(got[13])
        for k, value in enumerate(tensor_of(got[6], got[7:13])):
            es[l, k, rows, :] = value
        for k in range(3):
            m0[k, l, rows, :] = got[k] + got[3 + k]
        return 0

    lax.fori_loop(0, nl, layer, 0)
    for i, out in enumerate((ca, cb)):
        l = jnp.where(px == i, nl - 1, 0)
        for k in range(13):
            out[k] = pick(k, l).astype(BF16)


def strain_parts(c, n, ynext, znext):
    ax = [n[k] - c[k] for k in range(3)]
    ay = [ynext[k] - c[k] for k in range(3)]
    az = [znext[k] - c[k] for k in range(3)]
    return [ax[0], ay[1], az[2], ay[0] + ax[1], az[0] + ax[2], az[1] + ay[2]]


def stress(parts, tensor, which):
    two_eta, s = tensor[0], tensor[1:]
    cross = (
        (s[0] * parts[0] + s[1] * parts[1])
        + (s[2] * parts[2] + s[3] * parts[3])
        + (s[4] * parts[4] + s[5] * parts[5])
    )
    eta = 0.5 * two_eta
    return {k: (two_eta if k < 3 else eta) * parts[k] - cross * s[k] for k in which}


class Plane:
    def __init__(self, center, following, tensor, tiles):
        self.center, self.following, self.tensor, self.tiles = center, following, tensor, tiles
        self.row, self.lane = iotas()
        self.cache = {}

    def tile(self, t):
        if t not in self.cache:
            m = [[self.center(k, t, h) for k in range(3)] for h in range(2)]
            r = [[pltpu.roll(m[h][k], ROWS - 1, 0) for k in range(3)] for h in range(2)]
            self.cache = {k: v for k, v in self.cache.items() if k == (t - 1) % self.tiles}
            self.cache[t] = (m, r)
        return self.cache[t]

    def stresses(self, t, which):
        m, r = self.tile(t)
        _, rn = self.tile((t + 1) % self.tiles)
        z = [[pltpu.roll(m[h][k], LANES - 1, 1) for k in range(3)] for h in range(2)]
        out = []
        for h in range(2):
            ynext = [jnp.where(self.row == ROWS - 1, rn[h][k], r[h][k]) for k in range(3)]
            znext = [jnp.where(self.lane == LANES - 1, z[1][k] if h == 0 else 0.0, z[h][k]) for k in range(3)]
            n = [self.following(k, t, h) for k in range(3)]
            parts = strain_parts(m[h], n, ynext, znext)
            out.append(stress(parts, [self.tensor(k, t, h) for k in range(7)], which))
        return m, out


FLUX_X, FLUX_Y, FLUX_Z = (0, 3, 4), (3, 1, 5), (4, 5, 2)


def full_plane(plane, tx, weight, write, own):
    row, lane, tiles = plane.row, plane.lane, plane.tiles
    halo = tiles - 1
    before = None
    kept = None

    def flux(t):
        m, tau = plane.stresses(t, range(6))
        y = [[tau[h][j] for j in FLUX_Y] for h in range(2)]
        ry = [[pltpu.roll(v, 1, 0) for v in y[h]] for h in range(2)]
        rz = [[pltpu.roll(tau[h][j], 1, 1) for j in FLUX_Z] for h in range(2)]
        div = []
        for h in range(2):
            rows, cols = at(t, h)
            line = []
            for k in range(3):
                x = tau[h][FLUX_X[k]]
                prev_z = jnp.where(lane == 0, rz[0][k] if h == 1 else 0.0, rz[h][k])
                line.append((tx[k, rows, cols] - x) + (prev_z - tau[h][FLUX_Z[k]]) - y[h][k])
                tx[k, rows, cols] = x
            div.append(line)
        return m, ry, div

    def finish(t, m, ry, div, prev):
        for h in range(2):
            rows, cols = at(t, h)
            wt = weight(t, h)
            new = [
                jnp.where(
                    wt > 0.0,
                    div[h][k] + jnp.where(row == 0, prev[h][k], ry[h][k]) + wt * m[h][k],
                    0.0,
                )
                for k in range(3)
            ]
            for k in range(3):
                write(k, t, h, new[k])
            if t != halo and own is not None:
                own(t, h, m[h], new)

    kept = flux(halo)
    before = kept[1]
    for t in range(halo):
        m, ry, div = flux(t)
        finish(t, m, ry, div, before)
        before = ry
    finish(halo, kept[0], kept[1], kept[2], before)


def lower_flux(plane, emit):
    for t in range(plane.tiles):
        _, tau = plane.stresses(t, FLUX_X)
        for h in range(2):
            emit(t, h, [tau[h][j] for j in FLUX_X])


class Sums:
    def __init__(self, init):
        self.cross = list(init[0])
        self.square = list(init[1])

    def add(self, t, h, old, new):
        i = (2 * t + h) % len(self.cross)
        for k in range(3):
            self.cross[i] = self.cross[i] + old[k] * new[k]
            self.square[i] = self.square[i] + new[k] * new[k]

    def state(self):
        return (tuple(self.cross), tuple(self.square))


def interior_kernel(m, es, w, v, tx_out, acc):
    nl, tiles = m.shape[1], m.shape[2] // ROWS
    zero = jnp.zeros((ROWS, LANES), F32)
    tx_out[...] = jnp.zeros(tx_out.shape, F32)

    def layer(l, carry):
        sums = Sums(carry)
        plane = Plane(
            lambda k, t, h: m[(k, l) + at(t, h)],
            lambda k, t, h: m[(k, l + 1) + at(t, h)],
            lambda k, t, h: es[(l, k) + at(t, h)],
            tiles,
        )

        def write(k, t, h, value):
            v[(k, l) + at(t, h)] = value

        full_plane(plane, tx_out, lambda t, h: w[(l,) + at(t, h)], write, sums.add)
        keep = jnp.where(l > 0, 1.0, 0.0).astype(F32)
        return jax.tree.map(lambda s: s * keep, sums.state())

    start = ((zero, zero), (zero, zero))
    cross, square = lax.fori_loop(0, nl - 1, layer, start)
    acc[0] = cross[0] + cross[1]
    acc[1] = square[0] + square[1]


def boundary_body(px, m, es, w, lo, hi, low_tensor, v_in, tx_in, acc_in, v, tx, acc):
    nl, tiles = m.shape[1], m.shape[2] // ROWS
    last = nl - 1
    zero = jnp.zeros((ROWS, LANES), F32)
    sums = Sums(((zero, zero), (zero, zero)))

    below = Plane(lo, lambda k, t, h: m[(k, 0) + at(t, h)], low_tensor, tiles)

    def emit(t, h, flux):
        wt = w[(0,) + at(t, h)]
        new = []
        for k in range(3):
            value = v_in[(k, 0) + at(t, h)] + jnp.where(wt > 0.0, flux[k], 0.0)
            v[(k, 0) + at(t, h)] = value
            new.append(value)
        if t != tiles - 1:
            sums.add(t, h, [m[(k, 0) + at(t, h)] for k in range(3)], new)

    lower_flux(below, emit)
    for k in range(3):
        tx[k] = tx_in[k]
    top = Plane(
        lambda k, t, h: m[(k, last) + at(t, h)],
        hi,
        lambda k, t, h: es[(last, k) + at(t, h)],
        tiles,
    )

    def write(k, t, h, value):
        v[(k, last) + at(t, h)] = value

    full_plane(top, tx, lambda t, h: w[(last,) + at(t, h)], write, sums.add)
    acc[0] = acc_in[0] + sums.cross[0] + sums.cross[1]
    acc[1] = acc_in[1] + sums.square[0] + sums.square[1]


def choose(flag, a, b):
    return jnp.where(flag + jnp.zeros(a.shape, jnp.int32) == 1, a, b)


def send_planes(px, v, ea, eb):
    last = v.shape[1] - 1
    for i, out in enumerate((ea, eb)):
        l = jnp.where(px == i, last, 0)
        for k in range(3):
            out[k] = v[k, l]


def first_boundary_kernel(par, m, es, w, xa, xb, ca, cb, v_in, tx_in, acc_in, v, acc, low, ea, eb, lo_s, hi_s, tx):
    px = par[0]
    even = (px == 0).astype(jnp.int32)
    nrow = xa.shape[1]

    def unpack(a, b, rows, n):
        def side(k, up):
            x, y = a(k), b(k)
            return choose(even, x, y) if up else choose(even, y, x)

        for k in range(3):
            hi_s[k, rows, :] = side(k, True) + side(3 + k, True)
            lo_s[k, rows, :] = side(k, False) + side(3 + k, False)
        tensor = tensor_of(side(6, False), [side(7 + k, False) for k in range(6)])
        for k in range(7):
            low[k, rows, :] = tensor[k]

    for t in range(nrow // 16):
        rows = pl.ds(16 * t, 16)
        unpack(lambda k: xa[k, rows, :].astype(F32), lambda k: xb[k, rows, :].astype(F32), rows, 16)
    unpack(lambda k: ca[k].astype(F32), lambda k: cb[k].astype(F32), pl.ds(nrow, ROWS), ROWS)
    boundary_body(
        px, m, es, w,
        lambda k, t, h: lo_s[(k,) + at(t, h)],
        lambda k, t, h: hi_s[(k,) + at(t, h)],
        lambda k, t, h: low[(k,) + at(t, h)],
        v_in, tx_in, acc_in, v, tx, acc,
    )
    send_planes(px, v, ea, eb)


def later_boundary(par, m, es, w, low, ra, rb, v_in, tx_in, acc_in, v, acc, tx):
    px = par[0]
    even = (px == 0).astype(jnp.int32)
    lo = lambda k, t, h: choose(even, rb[(k,) + at(t, h)], ra[(k,) + at(t, h)])
    hi = lambda k, t, h: choose(even, ra[(k,) + at(t, h)], rb[(k,) + at(t, h)])
    boundary_body(px, m, es, w, lo, hi, lambda k, t, h: low[(k,) + at(t, h)], v_in, tx_in, acc_in, v, tx, acc)


def second_boundary_kernel(par, m, es, w, low, ra, rb, v_in, tx_in, acc_in, v, acc, ea, eb, tx):
    later_boundary(par, m, es, w, low, ra, rb, v_in, tx_in, acc_in, v, acc, tx)
    send_planes(par[0], v, ea, eb)


def third_boundary_kernel(
    par, m, es, w, low, ra, rb, v_in, tx_in, acc_in, acc0, acc1, acc2, v, parts, tx, acc
):
    later_boundary(par, m, es, w, low, ra, rb, v_in, tx_in, acc_in, v, acc, tx)
    _, lane = iotas()
    line = jnp.zeros((ROWS, LANES), F32)
    terms = [acc0[0], acc0[1], acc1[0], acc1[1], acc2[0], acc2[1], acc[0]]
    for i, value in enumerate(terms):
        total = jnp.sum(jnp.sum(value, axis=0, keepdims=True), axis=1, keepdims=True)
        line = jnp.where(lane == i, total, line)
    for t in range(parts.shape[0] // ROWS):
        parts[pl.ds(ROWS * t, ROWS), :] = line


def coefficients(moment):
    size = 4
    zero = None

    def dot(a, b, shift):
        total = None
        for i in range(size):
            for j in range(size):
                if a[i] is None or b[j] is None:
                    continue
                term = a[i] * b[j] * moment[i + j + shift]
                total = term if total is None else total + term
        return total

    def axpy(a, scale, b):
        out = []
        for x, y in zip(a, b):
            term = None if y is None else scale * y
            out.append(x if term is None else term if x is None else x + term)
        return out

    one = jnp.ones_like(moment[0])
    residual = [one, zero, zero, zero]
    direction = list(residual)
    field = [zero] * size
    now = moment[0]
    for iteration in range(3):
        alpha = now / dot(direction, direction, 1)
        field = axpy(field, alpha, direction)
        if iteration == 2:
            break
        residual = axpy(residual, -alpha, [None] + direction[: size - 1])
        following = dot(residual, residual, 0)
        direction = axpy(residual, following / now, direction)
        now = following
    return field[:3]


def output_kernel(gathered, raw, w, m1, m2, m3, x, r, xs, rs, sem):
    nl, nrow = raw.shape[1], raw.shape[2]
    total = jnp.sum(gathered[...], axis=0, keepdims=True)
    lane = lax.broadcasted_iota(jnp.int32, (1, LANES), 1)
    term = [
        jnp.broadcast_to(jnp.sum(jnp.where(lane == i, total, 0.0), axis=1, keepdims=True), (ROWS, LANES))
        for i in range(7)
    ]
    held = term[1]
    moment = [term[0] + held] + [term[i] + held for i in range(2, 7)]
    c = coefficients(moment)
    both = c[0] + c[1] + c[2]
    for l in range(nl):
        slot = l % 2
        copies = [
            pltpu.make_async_copy(xs.at[slot], x.at[:, l], sem.at[slot, 0]),
            pltpu.make_async_copy(rs.at[slot], r.at[:, l], sem.at[slot, 1]),
        ]
        if l >= 2:
            for copy in copies:
                copy.wait()

        def chunk(u, _):
            for i in range(4):
                for h in range(2):
                    rows = pl.ds(pl.multiple_of(ROWS * (4 * u + i), ROWS), ROWS)
                    cols = pl.ds(LANES * h, LANES)
                    free = w[l, rows, cols] > 0.0
                    fx = jnp.where(free, c[0], both)
                    fr = jnp.where(free, 1.0, 1.0 - both)
                    for k in range(3):
                        b = raw[k, l, rows, cols]
                        v1, v2, v3 = m1[k, l, rows, cols], m2[k, l, rows, cols], m3[k, l, rows, cols]
                        xs[slot, k, rows, cols] = fx * b + (c[1] * v1 + c[2] * v2)
                        rs[slot, k, rows, cols] = fr * b - (c[0] * v1 + c[1] * v2 + c[2] * v3)
            return 0

        lax.fori_loop(0, nrow // (4 * ROWS), chunk, 0)
        for copy in copies:
            copy.start()
    for l in range(max(0, nl - 2), nl):
        slot = l % 2
        pltpu.make_async_copy(xs.at[slot], x.at[:, l], sem.at[slot, 0]).wait()
        pltpu.make_async_copy(rs.at[slot], r.at[:, l], sem.at[slot, 1]).wait()


def exchange(x, axis, first):
    peers = lax.axis_size(axis)
    pairs = []
    for i in range(first, peers - 1, 2):
        pairs += [(i, i + 1), (i + 1, i)]
    return lax.ppermute(x, axis, pairs)


def per_device(b, visc, strain, code):
    _, nl, nrow, nz = b.shape
    rows = nrow + ROWS
    par = jnp.stack([lax.axis_index("gx") % 2, lax.axis_index("yz") % 2]).astype(jnp.int32)
    peers = lax.axis_size("gx") * lax.axis_size("yz")
    S = jax.ShapeDtypeStruct

    ya, yb, xa, xb = call(
        pack_kernel, "pack",
        [("smem", par), ("hbm", b), ("hbm", visc), ("hbm", strain), ("hbm", code)],
        [resident((14, nl, ROWS, nz), BF16)] * 2 + [resident((13, nrow, nz), BF16)] * 2,
        scratch=[
            VMEM((2, 3, nl, ROWS, nz), F32), VMEM((2, nl, ROWS, nz), BF16), VMEM((2, 6, nl, ROWS, nz), BF16),
            VMEM((2, nl, ROWS, nz), jnp.int32), VMEM((2, 3, nrow, nz), F32), VMEM((2, nrow, nz), jnp.int32),
            pltpu.SemaphoreType.DMA((2, 8)),
        ],
        cost=(1e6, 2e6),
    )
    rya, ryb = exchange(ya, "yz", 0), exchange(yb, "yz", 1)
    rxa, rxb = exchange(xa, "gx", 0), exchange(xb, "gx", 1)

    raw, es, m0, w, acc0 = call(
        load_kernel, "load",
        [("hbm", b), ("hbm", visc), ("hbm", strain), ("hbm", code)],
        [
            resident((3, nl, nrow, nz)), resident((nl, 7, rows, nz)), resident((3, nl, rows, nz)),
            resident((nl, rows, nz)), resident((2, ROWS, LANES)),
        ],
        scratch=[
            VMEM((nl, nrow, nz), BF16), VMEM((nl, 6, nrow, nz), BF16), VMEM((nl, nrow, nz), jnp.int32),
            pltpu.SemaphoreType.DMA((nl, 4)),
        ],
        cost=(2e7, 9e6),
    )
    es, m0, w, ca, cb = call(
        halo_kernel, "halo",
        [("smem", par), ("v", rya), ("v", ryb), ("v", es), ("v", m0), ("v", w)],
        [
            resident((nl, 7, rows, nz)), resident((3, nl, rows, nz)), resident((nl, rows, nz)),
            resident((13, ROWS, nz), BF16), resident((13, ROWS, nz), BF16),
        ],
        aliases={3: 0, 4: 1, 5: 2},
    )
    rca, rcb = exchange(ca, "gx", 0), exchange(cb, "gx", 1)

    field = resident((3, nl, rows, nz))
    sums = resident((2, ROWS, LANES))
    plane = resident((3, rows, nz))
    tx_scratch = VMEM((3, rows, nz), F32)
    work = (4e7, 1e7)

    v, tx, acc = call(
        interior_kernel, "interior1", [("v", m0), ("v", es), ("v", w)], [field, plane, sums], cost=work
    )
    m1, acc1, low, ea, eb = call(
        first_boundary_kernel, "boundary1",
        [("smem", par), ("v", m0), ("v", es), ("v", w), ("v", rxa), ("v", rxb), ("v", rca), ("v", rcb),
         ("v", v), ("v", tx), ("v", acc)],
        [field, sums, resident((7, rows, nz)), plane, plane],
        scratch=[tx_scratch, tx_scratch, tx_scratch],
        aliases={8: 0},
    )
    ra, rb = exchange(ea, "gx", 0), exchange(eb, "gx", 1)
    v, tx, acc = call(
        interior_kernel, "interior2", [("v", m1), ("v", es), ("v", w)], [field, plane, sums], cost=work
    )
    m2, acc2, ea, eb = call(
        second_boundary_kernel, "boundary2",
        [("smem", par), ("v", m1), ("v", es), ("v", w), ("v", low), ("v", ra), ("v", rb),
         ("v", v), ("v", tx), ("v", acc)],
        [field, sums, plane, plane],
        scratch=[tx_scratch],
        aliases={7: 0},
    )
    ra, rb = exchange(ea, "gx", 0), exchange(eb, "gx", 1)
    v, tx, acc = call(
        interior_kernel, "interior3", [("v", m2), ("v", es), ("v", w)], [field, plane, sums], cost=work
    )
    m3, parts = call(
        third_boundary_kernel, "boundary3",
        [("smem", par), ("v", m2), ("v", es), ("v", w), ("v", low), ("v", ra), ("v", rb),
         ("v", v), ("v", tx), ("v", acc), ("v", acc0), ("v", acc1), ("v", acc2)],
        [field, resident((peers, LANES))],
        scratch=[tx_scratch, VMEM((2, ROWS, LANES), F32)],
        aliases={7: 0},
    )
    gathered = lax.all_to_all(parts, ("gx", "yz"), 0, 0)
    return call(
        output_kernel, "output",
        [("v", gathered), ("v", raw), ("v", w), ("v", m1), ("v", m2), ("v", m3)],
        [S(b.shape, F32), S(b.shape, F32)],
        scratch=[VMEM((2, 3, nrow, nz), F32), VMEM((2, 3, nrow, nz), F32), pltpu.SemaphoreType.DMA((2, 2))],
    )


def solution(mesh):
    placed = (
        P(None, "gx", "yz", None),
        P("gx", "yz", None),
        P(None, "gx", "yz", None),
        P("gx", "yz", None),
    )
    return jax.shard_map(
        per_device,
        mesh=mesh,
        in_specs=placed,
        out_specs=(P(None, "gx", "yz", None), P(None, "gx", "yz", None)),
        check_vma=False,
    )
```

time: 454 us -> 89.1 us (0.20)
  blocking collectives: 329 us -> 23.7 us
  other arithmetic: 63.6 us -> 0.08 us
  Pallas kernels: 0 us -> 34.3 us
  starting transfers between devices: 30.5 us -> 20.1 us
  waiting for transfers between devices: 12.1 us -> 3.66 us
  between operations: 7.67 us -> 0.84 us
    psum x5 -> x0, blocking collectives: 329 us -> none  [the longest x3 197 us: squares(): return lax.psum(jnp.sum(vector * vector), ('gx', 'yz'))]
    pallas_call x0 -> x10, Pallas kernels: none -> 34.3 us  [call(): pl.pallas_call(kernel, name=name, out_shape=outs, in_specs=specs, out_spe...]
    all_to_all x0 -> x1, blocking collectives: none -> 23.7 us  [per_device(): gathered = lax.all_to_all(parts, ('gx', 'yz'), 0, 0)]
    reduce_sum x5 -> x0, other arithmetic: 22.5 us -> none  [the longest x3 13.1 us: per_device(): alpha = norm_now / lax.psum(jnp.sum(direction * image), ('gx', 'yz'))]
    sub x4 -> x0, other arithmetic: 16.9 us -> none  [the longest x1 9.53 us: per_device(): residual = residual - alpha * image]
    another operation x9 -> x1, other arithmetic: 12.7 us -> 0.08 us  [per_device(): jnp.stack([lax.axis_index('gx') % 2, lax.axis_index('yz') % 2])]
    ppermute x12 -> x10, starting transfers between devices: 30.5 us -> 20.1 us  [exchange(): return lax.ppermute(x, axis, pairs)]
    mul x3 -> x0, other arithmetic: 9.22 us -> none  [operate_shifts(): masked = mask * field]
  transfers between devices with their start and end apart: 12 -> 10, of which waited for: 11 -> 3; matrix products, arithmetic and copies ran while one was open for 2% -> 0% of each run, Pallas kernels for 0% -> 24%
where the time goes in v1:
time: 89.1 us; the launch traced here: 88.7 us
  Pallas kernels  34.3 us (38%)
  blocking collectives  23.7 us (27%)
  starting transfers between devices  20.1 us (23%)
  local copies, waits for them, and re-layouts  6.05 us (7%)
  waiting for transfers between devices  3.66 us (4%)
    pallas_call x10, Pallas kernels, call(): pl.pallas_call(kernel, name=name, out_shape=outs, in_specs=specs, out_spe...  34.3 us
    all_to_all x1, blocking collectives, per_device(): gathered = lax.all_to_all(parts, ('gx', 'yz'), 0, 0)  23.7 us
    ppermute x10, starting transfers between devices, exchange(): return lax.ppermute(x, axis, pairs)  20.1 us
    unnamed x14, local copies, waits for them, and re-layouts  6.05 us
    ppermute x10, waiting for transfers between devices, exchange(): return lax.ppermute(x, axis, pairs)  3.66 us
  transfers between devices with their start and end apart: 10, of which 3 were waited for; matrix products, arithmetic and copies ran while one was open for 0% of the time, Pallas kernels for 24%

profile of v1, /device:TPU:1, one launch (start us, length us, event | category | flops | bytes accessed | tf_op | source)
XLA Modules:
  0.0 88.7 jit_solution(5790342282448232668)
XLA Ops:
  0.7 1.9 %copy-done = f32[3,8,128,256]{3,2,1,0:T(8,128)S(1)} copy-done((f32[3,8,128,256]{3,2,1,0:T(8,128)S(1)}, f32[3,8,128,256]{3,2,1,0:T(8,128)}, u32[]{:S(2)}) %copy-start) | copy-done | bytes 3145752
  2.6 1.9 %copy-done.2 = bf16[6,8,128,256]{3,2,1,0:T(8,128)(2,1)S(1)} copy-done((bf16[6,8,128,256]{3,2,1,0:T(8,128)(2,1)S(1)}, bf16[6,8,128,256]{3,2,1,0:T(8,128)(2,1)}, u32[]{:S(2)}) %copy-start.2) | copy-done | bytes 3145752
  4.5 1.2 %copy-done.4 = s32[8,128,256]{2,1,0:T(8,128)S(1)} copy-done((s32[8,128,256]{2,1,0:T(8,128)S(1)}, s32[8,128,256]{2,1,0:T(8,128)}, u32[]{:S(2)}) %copy-start.4) | copy-done | bytes 1048600
  5.7 1.0 %copy-done.6 = bf16[8,128,256]{2,1,0:T(8,128)(2,1)S(1)} copy-done((bf16[8,128,256]{2,1,0:T(8,128)(2,1)S(1)}, bf16[8,128,256]{2,1,0:T(8,128)(2,1)}, u32[]{:S(2)}) %copy-start.6) | copy-done | bytes 524312
  6.8 1.8 %pack.1 = (bf16[14,8,8,256]{3,2,1,0:T(8,128)(2,1)S(1)}, bf16[14,8,8,256]{3,2,1,0:T(8,128)(2,1)S(1)}, bf16[13,128,256]{2,1,0:T(8,128)(2,1)S(1)}, bf16[13,128,256]{2,1,0:T(8,128)(2,1)S(1)}) custom-call(s32[2]{0:T(128)S(1)} %pad_add_fusion.par, f32[3,8,128,256]{3,2,1,0:T(8,128)S(1)} %copy-done, bf16[8,128,256]{2,1,0:T(8,128)(2,1)S(1)} %copy-done.6, ...), custom_call_target="tpu_custom_call" | custom-call | flops 1000000 | bytes 2000000 | tf_op jit(solution)/shard_map/pack/pallas_call | solution.py:40
  8.6 1.5 %collective-permute-start.2 = (bf16[13,128,256]{2,1,0:T(8,128)(2,1)S(1)}, bf16[13,128,256]{2,1,0:T(8,128)(2,1)S(1)}, u32[]{:S(2)}, u32[]{:S(2)}) collective-permute-start(bf16[13,128,256]{2,1,0:T(8,128)(2,1)S(1)} %get-tuple-element.44), channel_id=1, source_target_pairs={{0,16},{16,0},{32,48},{48,32},{64,80},{80,64},{96,112},{112,96},{1... | collective-permute-start | bytes 2555912 | tf_op jit(solution)/shard_map/ppermute | solution.py:552
  10.0 3.3 %collective-permute-start.3 = (bf16[13,128,256]{2,1,0:T(8,128)(2,1)S(1)}, bf16[13,128,256]{2,1,0:T(8,128)(2,1)S(1)}, u32[]{:S(2)}, u32[]{:S(2)}) collective-permute-start(bf16[13,128,256]{2,1,0:T(8,128)(2,1)S(1)} %get-tuple-element.45), channel_id=1, source_target_pairs={{16,32},{32,16},{48,64},{64,48},{80,96},{96,80},{17,33},{33,17},{4... | collective-permute-start | bytes 2555912 | tf_op jit(solution)/shard_map/ppermute | solution.py:552
  13.3 1.7 %collective-permute-start = (bf16[14,8,8,256]{3,2,1,0:T(8,128)(2,1)S(1)}, bf16[14,8,8,256]{3,2,1,0:T(8,128)(2,1)S(1)}, u32[]{:S(2)}, u32[]{:S(2)}) collective-permute-start(bf16[14,8,8,256]{3,2,1,0:T(8,128)(2,1)S(1)} %get-tuple-element.36), channel_id=1, source_target_pairs={{0,1},{1,0},{2,3},{3,2},{4,5},{5,4},{6,7},{7,6},{8,9},{9,8},{10,11... | collective-permute-start | bytes 1376264 | tf_op jit(solution)/shard_map/ppermute | solution.py:552
  15.7 5.9 %load.1 = (f32[3,8,128,256]{3,2,1,0:T(8,128)S(1)}, f32[8,7,136,256]{3,2,1,0:T(8,128)S(1)}, f32[3,8,136,256]{3,2,1,0:T(8,128)S(1)}, f32[8,136,256]{2,1,0:T(8,128)S(1)}, f32[2,8,128]{2,1,0:T(8,128)S(1)}) custom-call(f32[3,8,128,256]{3,2,1,0:T(8,128)S(1)} %copy-done.1, bf16[8,128,256]{2,1,0:T(8,128)(2,1)S(1)} %copy-done.6, ...), custom_call_target="tpu_custom_call" | custom-call | flops 20000000 | bytes 9000000 | tf_op jit(solution)/shard_map/load/pallas_call | solution.py:40
  21.7 2.0 %collective-permute-done.ra = bf16[14,8,8,256]{3,2,1,0:T(8,128)(2,1)S(1)} collective-permute-done((bf16[14,8,8,256]{3,2,1,0:T(8,128)(2,1)S(1)}, bf16[14,8,8,256]{3,2,1,0:T(8,128)(2,1)S(1)}, u32[]{:S(2)}, u32[]{:S(2)}) %collective-permute-start) | collective-permute-done | bytes 458784 | tf_op jit(solution)/shard_map/ppermute | solution.py:552
  23.7 0.9 %halo.1 = (f32[8,7,136,256]{3,2,1,0:T(8,128)S(1)}, f32[3,8,136,256]{3,2,1,0:T(8,128)S(1)}, f32[8,136,256]{2,1,0:T(8,128)S(1)}, bf16[13,8,256]{2,1,0:T(8,128)(2,1)S(1)}, bf16[13,8,256]{2,1,0:T(8,128)(2,1)S(1)}) custom-call(s32[2]{0:T(128)S(1)} %pad_add_fusion.par, ...), custom_call_target="tpu_custom_call", output_to_operand_aliasing={{0}: (3, {}), {1}: (4, {}), {2}: (5, {})} | custom-call | flops 1000000 | bytes 1000000 | tf_op jit(solution)/shard_map/halo/pallas_call | solution.py:40
  24.7 5.2 %collective-permute-start.5 = (bf16[13,8,256]{2,1,0:T(8,128)(2,1)S(1)}, bf16[13,8,256]{2,1,0:T(8,128)(2,1)S(1)}, u32[]{:S(2)}, u32[]{:S(2)}) collective-permute-start(bf16[13,8,256]{2,1,0:T(8,128)(2,1)S(1)} %get-tuple-element.47), channel_id=1, source_target_pairs={{16,32},{32,16},{48,64},{64,48},{80,96},{96,80},{17,33},{33,17},{4... | collective-permute-start | bytes 159752 | tf_op jit(solution)/shard_map/ppermute | solution.py:552
  29.9 4.8 %interior1.1 = (f32[3,8,136,256]{3,2,1,0:T(8,128)S(1)}, f32[3,136,256]{2,1,0:T(8,128)S(1)}, f32[2,8,128]{2,1,0:T(8,128)S(1)}) custom-call(f32[3,8,136,256]{3,2,1,0:T(8,128)S(1)} %get-tuple-element.41.m, f32[8,7,136,256]{3,2,1,0:T(8,128)S(1)} %get-tuple-element.42.es, f32[8,136,256]{2,1,0:T(8,128)S(1)} %get-tuple-element.43.w), custom_call_target="tpu_custom_call" | custom-call | flops 40000000 | bytes 10000000 | tf_op jit(solution)/shard_map/interior1/pallas_call | solution.py:40
  34.8 2.3 %boundary1.1 = (f32[3,8,136,256]{3,2,1,0:T(8,128)S(1)}, f32[2,8,128]{2,1,0:T(8,128)S(1)}, f32[7,136,256]{2,1,0:T(8,128)S(1)}, f32[3,136,256]{2,1,0:T(8,128)S(1)}, f32[3,136,256]{2,1,0:T(8,128)S(1)}) custom-call(s32[2]{0:T(128)S(1)} %pad_add_fusion.par, f32[3,8,136,256]{3,2,1,0:T(8,128)S(1)} %get-tuple-element.41.m, ...), custom_call_target="tpu_custom_call", output_to_operand_aliasing={{0}: (8, {})} | custom-call | flops 1000000 | bytes 1000000 | tf_op jit(solution)/shard_map/boundary1/pallas_call | solution.py:40
  37.2 3.9 %collective-permute-start.7 = (f32[3,136,256]{2,1,0:T(8,128)S(1)}, f32[3,136,256]{2,1,0:T(8,128)S(1)}, u32[]{:S(2)}, u32[]{:S(2)}) collective-permute-start(f32[3,136,256]{2,1,0:T(8,128)S(1)} %get-tuple-element.54), channel_id=1, source_target_pairs={{16,32},{32,16},{48,64},{64,48},{80,96},{96,80},{17,33},{33,17},{4... | collective-permute-start | bytes 1253384 | tf_op jit(solution)/shard_map/ppermute | solution.py:552
  41.1 4.8 %interior2.1 = (f32[3,8,136,256]{3,2,1,0:T(8,128)S(1)}, f32[3,136,256]{2,1,0:T(8,128)S(1)}, f32[2,8,128]{2,1,0:T(8,128)S(1)}) custom-call(f32[3,8,136,256]{3,2,1,0:T(8,128)S(1)} %get-tuple-element.51.m.m1, f32[8,7,136,256]{3,2,1,0:T(8,128)S(1)} %get-tuple-element.42.es, f32[8,136,256]{2,1,0:T(8,128)S(1)} %get-tuple-element.43.w), custom_call_target="tpu_custom_call" | custom-call | flops 40000000 | bytes 10000000 | tf_op jit(solution)/shard_map/interior2/pallas_call | solution.py:40
  46.0 0.9 collective-permute-done.7.rb
  46.8 2.1 %boundary2.1 = (f32[3,8,136,256]{3,2,1,0:T(8,128)S(1)}, f32[2,8,128]{2,1,0:T(8,128)S(1)}, f32[3,136,256]{2,1,0:T(8,128)S(1)}, f32[3,136,256]{2,1,0:T(8,128)S(1)}) custom-call(s32[2]{0:T(128)S(1)} %pad_add_fusion.par, f32[3,8,136,256]{3,2,1,0:T(8,128)S(1)} %get-tuple-element.51.m.m1, ...), custom_call_target="tpu_custom_call", output_to_operand_aliasing={{0}: (7, {})} | custom-call | flops 1000000 | bytes 1000000 | tf_op jit(solution)/shard_map/boundary2/pallas_call | solution.py:40
  49.0 3.7 %collective-permute-start.9 = (f32[3,136,256]{2,1,0:T(8,128)S(1)}, f32[3,136,256]{2,1,0:T(8,128)S(1)}, u32[]{:S(2)}, u32[]{:S(2)}) collective-permute-start(f32[3,136,256]{2,1,0:T(8,128)S(1)} %get-tuple-element.60), channel_id=1, source_target_pairs={{16,32},{32,16},{48,64},{64,48},{80,96},{96,80},{17,33},{33,17},{4... | collective-permute-start | bytes 1253384 | tf_op jit(solution)/shard_map/ppermute | solution.py:552
  52.7 4.9 %interior3.1 = (f32[3,8,136,256]{3,2,1,0:T(8,128)S(1)}, f32[3,136,256]{2,1,0:T(8,128)S(1)}, f32[2,8,128]{2,1,0:T(8,128)S(1)}) custom-call(f32[3,8,136,256]{3,2,1,0:T(8,128)S(1)} %get-tuple-element.58.m.m2, f32[8,7,136,256]{3,2,1,0:T(8,128)S(1)} %get-tuple-element.42.es, f32[8,136,256]{2,1,0:T(8,128)S(1)} %get-tuple-element.43.w), custom_call_target="tpu_custom_call" | custom-call | flops 40000000 | bytes 10000000 | tf_op jit(solution)/shard_map/interior3/pallas_call | solution.py:40
  57.7 0.8 collective-permute-done.9.rb
  58.4 1.8 %boundary3.1 = (f32[3,8,136,256]{3,2,1,0:T(8,128)S(1)}, f32[128,128]{1,0:T(8,128)S(1)}) custom-call(s32[2]{0:T(128)S(1)} %pad_add_fusion.par, f32[3,8,136,256]{3,2,1,0:T(8,128)S(1)} %get-tuple-element.58.m.m2, f32[8,7,136,256]{3,2,1,0:T(8,128)S(1)} %get-tuple-element.42.es, f32[8,136,256]{2,1,0:T(8,128)S(1)} %get-tuple-element.43.w, ...), custom_call_target="tpu_custom_call", output_to_operand_aliasing={{0}: (7, {})} | custom-call | flops 1000000 | bytes 1000000 | tf_op jit(solution)/shard_map/boundary3/pallas_call | solution.py:40
  60.3 23.7 %all_to_all.11 = f32[128,1,128]{2,1,0:T(1,128)S(1)} all-to-all(f32[128,1,128]{2,1,0:T(1,128)S(1)} %bitcast.7), channel_id=1, replica_groups=mesh['gx'=8,'yz'=16] {'gx','yz'}, dimensions={0} | all-to-all | bytes 131072 | tf_op jit(solution)/shard_map/all_to_all | solution.py:641
  83.9 4.8 %output.1 = (f32[3,8,128,256]{3,2,1,0:T(8,128)}, f32[3,8,128,256]{3,2,1,0:T(8,128)}) custom-call(f32[128,128]{1,0:T(8,128)S(1)} %bitcast.6, f32[3,8,128,256]{3,2,1,0:T(8,128)S(1)} %get-tuple-element.68.raw, f32[8,136,256]{2,1,0:T(8,128)S(1)} %get-tuple-element.43.w, f32[3,8,136,256]{3,2,1,0:T(8,128)S(1)} %get-tuple-element.51.m.m1, ...), custom_call_target="tpu_custom_call" | custom-call | flops 1000000 | bytes 1000000 | tf_op jit(solution)/shard_map/output/pallas_call | solution.py:40
  (22 shorter events, 1.0 us)
Async XLA Ops:
  0.7 1.9 %copy-start = (f32[3,8,128,256]{3,2,1,0:T(8,128)S(1)}, f32[3,8,128,256]{3,2,1,0:T(8,128)}, u32[]{:S(2)}) copy-start(f32[3,8,128,256]{3,2,1,0:T(8,128)} %b.3) | copy-start | bytes 9437188
  2.6 1.9 %copy-start.2 = (bf16[6,8,128,256]{3,2,1,0:T(8,128)(2,1)S(1)}, bf16[6,8,128,256]{3,2,1,0:T(8,128)(2,1)}, u32[]{:S(2)}) copy-start(bf16[6,8,128,256]{3,2,1,0:T(8,128)(2,1)} %strain.3) | copy-start | bytes 9437188
  4.5 1.2 %copy-start.4 = (s32[8,128,256]{2,1,0:T(8,128)S(1)}, s32[8,128,256]{2,1,0:T(8,128)}, u32[]{:S(2)}) copy-start(s32[8,128,256]{2,1,0:T(8,128)} %code.3) | copy-start | bytes 3145732
  5.7 1.0 %copy-start.6 = (bf16[8,128,256]{2,1,0:T(8,128)(2,1)S(1)}, bf16[8,128,256]{2,1,0:T(8,128)(2,1)}, u32[]{:S(2)}) copy-start(bf16[8,128,256]{2,1,0:T(8,128)(2,1)} %visc.3) | copy-start | bytes 1572868
  6.8 8.9 %copy-start.1 = (f32[3,8,128,256]{3,2,1,0:T(8,128)S(1)}, f32[3,8,128,256]{3,2,1,0:T(8,128)}, u32[]{:S(2)}) copy-start(f32[3,8,128,256]{3,2,1,0:T(8,128)} %b.3) | copy-start | bytes 9437188
  6.8 8.9 %copy-start.3 = (bf16[6,8,128,256]{3,2,1,0:T(8,128)(2,1)S(1)}, bf16[6,8,128,256]{3,2,1,0:T(8,128)(2,1)}, u32[]{:S(2)}) copy-start(bf16[6,8,128,256]{3,2,1,0:T(8,128)(2,1)} %strain.3) | copy-start | bytes 9437188
  6.8 8.9 %copy-start.5 = (s32[8,128,256]{2,1,0:T(8,128)S(1)}, s32[8,128,256]{2,1,0:T(8,128)}, u32[]{:S(2)}) copy-start(s32[8,128,256]{2,1,0:T(8,128)} %code.3) | copy-start | bytes 3145732
  8.6 26.2 %collective-permute-start.2 = (bf16[13,128,256]{2,1,0:T(8,128)(2,1)S(1)}, bf16[13,128,256]{2,1,0:T(8,128)(2,1)S(1)}, u32[]{:S(2)}, u32[]{:S(2)}) collective-permute-start(bf16[13,128,256]{2,1,0:T(8,128)(2,1)S(1)} %get-tuple-element.44), channel_id=1, source_target_pairs={{0,16},{16,0},{32,48},{48,32},{64,80},{80,64},{96,112},{112,96},{1... | collective-permute-start | bytes 2555912 | tf_op jit(solution)/shard_map/ppermute | solution.py:552
  10.0 24.8 %collective-permute-start.3 = (bf16[13,128,256]{2,1,0:T(8,128)(2,1)S(1)}, bf16[13,128,256]{2,1,0:T(8,128)(2,1)S(1)}, u32[]{:S(2)}, u32[]{:S(2)}) collective-permute-start(bf16[13,128,256]{2,1,0:T(8,128)(2,1)S(1)} %get-tuple-element.45), channel_id=1, source_target_pairs={{16,32},{32,16},{48,64},{64,48},{80,96},{96,80},{17,33},{33,17},{4... | collective-permute-start | bytes 2555912 | tf_op jit(solution)/shard_map/ppermute | solution.py:552
  13.3 10.4 %collective-permute-start = (bf16[14,8,8,256]{3,2,1,0:T(8,128)(2,1)S(1)}, bf16[14,8,8,256]{3,2,1,0:T(8,128)(2,1)S(1)}, u32[]{:S(2)}, u32[]{:S(2)}) collective-permute-start(bf16[14,8,8,256]{3,2,1,0:T(8,128)(2,1)S(1)} %get-tuple-element.36), channel_id=1, source_target_pairs={{0,1},{1,0},{2,3},{3,2},{4,5},{5,4},{6,7},{7,6},{8,9},{9,8},{10,11... | collective-permute-start | bytes 1376264 | tf_op jit(solution)/shard_map/ppermute | solution.py:552
  15.0 8.7 %collective-permute-start.1 = (bf16[14,8,8,256]{3,2,1,0:T(8,128)(2,1)S(1)}, bf16[14,8,8,256]{3,2,1,0:T(8,128)(2,1)S(1)}, u32[]{:S(2)}, u32[]{:S(2)}) collective-permute-start(bf16[14,8,8,256]{3,2,1,0:T(8,128)(2,1)S(1)} %get-tuple-element.37), channel_id=1, source_target_pairs={{1,2},{2,1},{3,4},{4,3},{5,6},{6,5},{7,8},{8,7},{9,10},{10,9},{11,... | collective-permute-start | bytes 1376264 | tf_op jit(solution)/shard_map/ppermute | solution.py:552
  24.6 10.1 %collective-permute-start.4 = (bf16[13,8,256]{2,1,0:T(8,128)(2,1)S(1)}, bf16[13,8,256]{2,1,0:T(8,128)(2,1)S(1)}, u32[]{:S(2)}, u32[]{:S(2)}) collective-permute-start(bf16[13,8,256]{2,1,0:T(8,128)(2,1)S(1)} %get-tuple-element.46), channel_id=1, source_target_pairs={{0,16},{16,0},{32,48},{48,32},{64,80},{80,64},{96,112},{112,96},{1... | collective-permute-start | bytes 159752 | tf_op jit(solution)/shard_map/ppermute | solution.py:552
  24.7 10.0 %collective-permute-start.5 = (bf16[13,8,256]{2,1,0:T(8,128)(2,1)S(1)}, bf16[13,8,256]{2,1,0:T(8,128)(2,1)S(1)}, u32[]{:S(2)}, u32[]{:S(2)}) collective-permute-start(bf16[13,8,256]{2,1,0:T(8,128)(2,1)S(1)} %get-tuple-element.47), channel_id=1, source_target_pairs={{16,32},{32,16},{48,64},{64,48},{80,96},{96,80},{17,33},{33,17},{4... | collective-permute-start | bytes 159752 | tf_op jit(solution)/shard_map/ppermute | solution.py:552
  37.1 8.8 %collective-permute-start.6 = (f32[3,136,256]{2,1,0:T(8,128)S(1)}, f32[3,136,256]{2,1,0:T(8,128)S(1)}, u32[]{:S(2)}, u32[]{:S(2)}) collective-permute-start(f32[3,136,256]{2,1,0:T(8,128)S(1)} %get-tuple-element.53), channel_id=1, source_target_pairs={{0,16},{16,0},{32,48},{48,32},{64,80},{80,64},{96,112},{112,96},{1... | collective-permute-start | bytes 1253384 | tf_op jit(solution)/shard_map/ppermute | solution.py:552
  37.2 9.6 %collective-permute-start.7 = (f32[3,136,256]{2,1,0:T(8,128)S(1)}, f32[3,136,256]{2,1,0:T(8,128)S(1)}, u32[]{:S(2)}, u32[]{:S(2)}) collective-permute-start(f32[3,136,256]{2,1,0:T(8,128)S(1)} %get-tuple-element.54), channel_id=1, source_target_pairs={{16,32},{32,16},{48,64},{64,48},{80,96},{96,80},{17,33},{33,17},{4... | collective-permute-start | bytes 1253384 | tf_op jit(solution)/shard_map/ppermute | solution.py:552
  48.9 8.8 %collective-permute-start.8 = (f32[3,136,256]{2,1,0:T(8,128)S(1)}, f32[3,136,256]{2,1,0:T(8,128)S(1)}, u32[]{:S(2)}, u32[]{:S(2)}) collective-permute-start(f32[3,136,256]{2,1,0:T(8,128)S(1)} %get-tuple-element.59), channel_id=1, source_target_pairs={{0,16},{16,0},{32,48},{48,32},{64,80},{80,64},{96,112},{112,96},{1... | collective-permute-start | bytes 1253384 | tf_op jit(solution)/shard_map/ppermute | solution.py:552
  49.0 9.4 %collective-permute-start.9 = (f32[3,136,256]{2,1,0:T(8,128)S(1)}, f32[3,136,256]{2,1,0:T(8,128)S(1)}, u32[]{:S(2)}, u32[]{:S(2)}) collective-permute-start(f32[3,136,256]{2,1,0:T(8,128)S(1)} %get-tuple-element.60), channel_id=1, source_target_pairs={{16,32},{32,16},{48,64},{64,48},{80,96},{96,80},{17,33},{33,17},{4... | collective-permute-start | bytes 1253384 | tf_op jit(solution)/shard_map/ppermute | solution.py:552

commit v2 on v1

--- a/solution.py
+++ b/solution.py
@@ -1,3 +1,5 @@
+import functools
+
 import jax
 import jax.numpy as jnp
 from jax import lax
@@ -5,11 +7,13 @@
 from jax.experimental.pallas import tpu as pltpu
 from jax.sharding import PartitionSpec as P
 
+
 SOFTEN = 0.8
 F32 = jnp.float32
 BF16 = jnp.bfloat16
 LANES = 128
 ROWS = 8
+HALO = 3
 VMEM = pltpu.VMEM
 
 
@@ -21,12 +25,12 @@
     return pltpu.with_memory_space_constraint(x, VMEM)
 
 
-def call(kernel, name, ins, outs, scratch=(), aliases=None, limit=24, cost=(1e6, 1e6)):
+def call(kernel, ins, outs, scratch=(), aliases=None, limit=24, cost=(1e6, 1e6)):
     specs, args = [], []
     for kind, x in ins:
         if kind == "hbm":
-            specs.append(pl.BlockSpec(memory_space=pl.ANY))
-            args.append(x)
+            specs.append(pl.BlockSpec(memory_space=pltpu.HBM))
+            args.append(pltpu.with_memory_space_constraint(x, pltpu.HBM))
         elif kind == "smem":
             specs.append(pl.BlockSpec(memory_space=pltpu.SMEM))
             args.append(x)
@@ -34,12 +38,11 @@
             specs.append(pl.BlockSpec(memory_space=VMEM))
             args.append(in_vmem(x))
     out_specs = [
-        pl.BlockSpec(memory_space=VMEM) if isinstance(o, type(VMEM((8, 128), F32))) else pl.BlockSpec(memory_space=pl.ANY)
+        pl.BlockSpec(memory_space=VMEM) if isinstance(o, type(VMEM((8, 128), F32))) else pl.BlockSpec(memory_space=pltpu.HBM)
         for o in outs
     ]
     return pl.pallas_call(
         kernel,
-        name=name,
         out_shape=outs,
         in_specs=specs,
         out_specs=out_specs,
@@ -81,8 +84,9 @@
     return high, (x - high.astype(F32)).astype(BF16)
 
 
-def pack_kernel(par, b, visc, strain, code, ya, yb, xa, xb, tb, tv, ts, tc, lb, lc, sem):
+def pack_y_kernel(par, b, visc, strain, code, ya, yb, token, tb, tv, ts, tc, sem):
     nl, nrow = b.shape[1], b.shape[2]
+    py = par[1]
     copies = []
     for i, r in enumerate((0, nrow - ROWS)):
         rows = pl.ds(r, ROWS)
@@ -90,8 +94,49 @@
         copies.append(pltpu.make_async_copy(visc.at[:, rows, :], tv.at[i], sem.at[i, 1]))
         copies.append(pltpu.make_async_copy(strain.at[:, :, rows, :], ts.at[i], sem.at[i, 2]))
         copies.append(pltpu.make_async_copy(code.at[:, rows, :], tc.at[i], sem.at[i, 3]))
+    for c in copies:
+        c.start()
+    token[...] = jnp.zeros(token.shape, F32)
+    for c in copies:
+        c.wait()
+    row, _ = iotas()
+    even = (py == 0).astype(jnp.int32) + jnp.zeros((ROWS, LANES), jnp.int32) == 1
+
+    def layer(l, _):
+        for h in range(2):
+            cols = pl.ds(LANES * h, LANES)
+            first, last = [], []
+            for slot, planes in ((0, first), (1, last)):
+                held = tc[slot, l, :, cols] == 0
+                b3 = [split(jnp.where(held, 0.0, tb[slot, k, l, :, cols])) for k in range(3)]
+                planes += [x[0].astype(F32) for x in b3] + [x[1].astype(F32) for x in b3]
+                planes.append(tv[slot, l, :, cols].astype(F32))
+                planes += [ts[slot, k, l, :, cols].astype(F32) for k in range(6)]
+                planes.append(tc[slot, l, :, cols].astype(F32))
+            last = [pltpu.roll(x, HALO, 0) for x in last]
+            for out, up in ((ya, True), (yb, False)):
+                planes = [jnp.where(even == up, y, x) for x, y in zip(first, last)]
+                for j in range(3):
+                    halves = []
+                    for tile in (2 * j, 2 * j + 1):
+                        value = jnp.zeros((ROWS, LANES), F32)
+                        for k, x in enumerate(planes):
+                            start = HALO * k - ROWS * tile
+                            if start <= -HALO or start >= ROWS:
+                                continue
+                            moved = pltpu.roll(x, start % ROWS, 0) if start % ROWS else x
+                            value = jnp.where((row >= start) & (row < start + HALO), moved, value)
+                        halves.append(value)
+                    out[l, pl.ds(16 * j, 16), cols] = jnp.concatenate(halves, 0).astype(BF16)
+        return 0
+
+    lax.fori_loop(0, nl, layer, 0)
+
+
+def pack_x_kernel(par, b, visc, strain, code, token, xa, xb, lb, lc, sem):
+    nl, nrow = b.shape[1], b.shape[2]
     px = par[0]
-    py = par[1]
+    copies = []
     late = []
     for i, out in enumerate((xa, xb)):
         layer = jnp.where(px == i, nl - 1, 0)
@@ -103,18 +148,6 @@
         c.start()
     for c in copies:
         c.wait()
-    for i, out in enumerate((ya, yb)):
-        slot = jnp.where(py == i, 1, 0)
-        for l in range(nl):
-            held = tc[slot, l] == 0
-            for k in range(3):
-                high, low = split(jnp.where(held, 0.0, tb[slot, k, l]))
-                out[k, l] = high
-                out[3 + k, l] = low
-            out[6, l] = tv[slot, l]
-            for k in range(6):
-                out[7 + k, l] = ts[slot, k, l]
-            out[13, l] = tc[slot, l].astype(F32).astype(BF16)
     for i, out in enumerate((xa, xb)):
         for t in range(nrow // 16):
             rows = pl.ds(16 * t, 16)
@@ -129,82 +162,99 @@
 
 def load_kernel(b, visc, strain, code, raw, es, m0, w, acc, sv, ss, sc, sem):
     nl, nrow = b.shape[1], b.shape[2]
-    copies = []
+
+    def copies(l):
+        return [
+            pltpu.make_async_copy(b.at[:, l], raw.at[:, l], sem.at[l, 0]),
+            pltpu.make_async_copy(visc.at[l], sv.at[l], sem.at[l, 1]),
+            pltpu.make_async_copy(strain.at[:, l], ss.at[l], sem.at[l, 2]),
+            pltpu.make_async_copy(code.at[l], sc.at[l], sem.at[l, 3]),
+        ]
+
     for l in range(nl):
-        copies.append(
-            [
-                pltpu.make_async_copy(b.at[:, l], raw.at[:, l], sem.at[l, 0]),
-                pltpu.make_async_copy(visc.at[l], sv.at[l], sem.at[l, 1]),
-                pltpu.make_async_copy(strain.at[:, l], ss.at[l], sem.at[l, 2]),
-                pltpu.make_async_copy(code.at[l], sc.at[l], sem.at[l, 3]),
-            ]
-        )
-        for c in copies[-1]:
+        for c in copies(l):
             c.start()
     zero = jnp.zeros((ROWS, LANES), F32)
 
-    def chunk(l, u, carry):
-        sums, helds = carry
-        base = pl.multiple_of(16 * u, 16)
-        rows16 = pl.ds(base, 16)
-        v16 = sv[l, rows16, :].astype(F32)
-        s16 = [ss[l, k, rows16, :].astype(F32) for k in range(6)]
-        for i in range(2):
-            for h in range(2):
-                cut = lambda x: x[ROWS * i : ROWS * (i + 1), LANES * h : LANES * (h + 1)]
-                rows, cols = pl.ds(pl.multiple_of(base + ROWS * i, ROWS), ROWS), pl.ds(LANES * h, LANES)
-                weight = weight_of(sc[l, rows, cols])
-                w[l, rows, cols] = weight
-                for k, value in enumerate(tensor_of(cut(v16), [cut(s) for s in s16])):
-                    es[l, k, rows, cols] = value
-                for k in range(3):
-                    x = raw[k, l, rows, cols]
-                    m = jnp.where(weight > 0.0, x, 0.0)
-                    m0[k, l, rows, cols] = m
-                    rest = x - m
-                    sums = sums + m * m
-                    helds = helds + rest * rest
-        return sums, helds
-
-    carry = (zero, zero)
-    for l in range(nl):
-        for c in copies[l]:
+    def layer(l, carry):
+        whole, held = list(carry[0]), list(carry[1])
+        for c in copies(l):
             c.wait()
-        carry = lax.fori_loop(0, nrow // 16, lambda u, s: chunk(l, u, s), carry)
-    acc[0] = carry[0]
-    acc[1] = carry[1]
+        for u in range(nrow // 16):
+            rows16 = pl.ds(16 * u, 16)
+            v16 = sv[l, rows16, :].astype(F32)
+            s16 = [ss[l, k, rows16, :].astype(F32) for k in range(6)]
+            for i in range(2):
+                for h in range(2):
+                    cut = lambda x: x[ROWS * i : ROWS * (i + 1), LANES * h : LANES * (h + 1)]
+                    rows, cols = pl.ds(16 * u + ROWS * i, ROWS), pl.ds(LANES * h, LANES)
+                    weight = weight_of(sc[l, rows, cols])
+                    w[l, rows, cols] = weight
+                    for k, value in enumerate(tensor_of(cut(v16), [cut(s) for s in s16])):
+                        es[l, k, rows, cols] = value
+                    x = [raw[k, l, rows, cols] for k in range(3)]
+                    for k in range(3):
+                        m0[k, l, rows, cols] = jnp.where(weight > 0.0, x[k], 0.0)
+                    square = x[0] * x[0] + x[1] * x[1] + x[2] * x[2]
+                    j = 2 * i + h
+                    whole[j] = whole[j] + square
+                    held[j] = held[j] + jnp.where(weight > 0.0, 0.0, square)
+        return tuple(whole), tuple(held)
+
+    whole, held = lax.fori_loop(0, nl, layer, ((zero,) * 4, (zero,) * 4))
+    acc[0] = (whole[0] + whole[1]) + (whole[2] + whole[3])
+    acc[1] = (held[0] + held[1]) + (held[2] + held[3])
 
 
 def halo_kernel(par, ra, rb, es_in, m0_in, w_in, es, m0, w, ca, cb):
-    row, _ = iotas()
+    _, _ = iotas()
     row2 = lax.broadcasted_iota(jnp.int32, (ROWS, 2 * LANES), 0)
-    nl = ra.shape[1]
+    nl = ra.shape[0]
     halo = es.shape[2] - ROWS
     px = par[0]
     py = par[1]
     rows = pl.ds(halo, ROWS)
 
-    def pick(k, l):
-        a, c = ra[k, l].astype(F32), rb[k, l].astype(F32)
-        even = (py == 0).astype(jnp.int32) + jnp.zeros_like(row2)
-        upper = jnp.where(even == 1, a, c)
-        lower = jnp.where(even == 1, c, a)
-        return jnp.where(row2 < 3, upper, jnp.where(row2 >= 5, lower, 0.0))
+    def planes(l):
+        a, c = ra[l].astype(F32), rb[l].astype(F32)
+        upper, lower = jnp.where(even3(a), a, c), jnp.where(even3(a), c, a)
+
+        def moved(x, k, to):
+            t, at_row = divmod(HALO * k, ROWS)
+            part = x[ROWS * t : ROWS * (t + 1)]
+            shift = (to - at_row) % ROWS
+            part = pltpu.roll(part, shift, 0) if shift else part
+            if at_row + HALO > ROWS:
+                following = x[ROWS * (t + 1) : ROWS * (t + 2)]
+                following = pltpu.roll(following, shift, 0) if shift else following
+                part = jnp.where(row2 - to >= ROWS - at_row, following, part)
+            return part
+
+        return [
+            jnp.where(row2 < HALO, moved(upper, k, 0), jnp.where(row2 >= ROWS - HALO, moved(lower, k, ROWS - HALO), 0.0))
+            for k in range(14)
+        ]
+
+    def even3(x):
+        return (py == 0).astype(jnp.int32) + jnp.zeros(x.shape, jnp.int32) == 1
 
     def layer(l, _):
-        got = [pick(k, l) for k in range(14)]
+        got = planes(l)
         w[l, rows, :] = weight_of(got[13])
         for k, value in enumerate(tensor_of(got[6], got[7:13])):
             es[l, k, rows, :] = value
         for k in range(3):
             m0[k, l, rows, :] = got[k] + got[3 + k]
+        for i, out in enumerate((ca, cb)):
+
+            @pl.when(l == jnp.where(px == i, nl - 1, 0))
+            def _():
+                for k in range(13):
+                    out[k] = got[k].astype(BF16)
+
         return 0
 
     lax.fori_loop(0, nl, layer, 0)
-    for i, out in enumerate((ca, cb)):
-        l = jnp.where(px == i, nl - 1, 0)
-        for k in range(13):
-            out[k] = pick(k, l).astype(BF16)
 
 
 def strain_parts(c, n, ynext, znext):
@@ -231,17 +281,15 @@
         self.row, self.lane = iotas()
         self.cache = {}
 
-    def tile(self, t):
+    def rolled(self, t):
         if t not in self.cache:
-            m = [[self.center(k, t, h) for k in range(3)] for h in range(2)]
-            r = [[pltpu.roll(m[h][k], ROWS - 1, 0) for k in range(3)] for h in range(2)]
-            self.cache = {k: v for k, v in self.cache.items() if k == (t - 1) % self.tiles}
-            self.cache[t] = (m, r)
+            self.cache[t] = [[pltpu.roll(self.center(k, t, h), ROWS - 1, 0) for k in range(3)] for h in range(2)]
         return self.cache[t]
 
     def stresses(self, t, which):
-        m, r = self.tile(t)
-        _, rn = self.tile((t + 1) % self.tiles)
+        m = [[self.center(k, t, h) for k in range(3)] for h in range(2)]
+        r, rn = self.rolled(t), self.rolled((t + 1) % self.tiles)
+        del self.cache[t]
         z = [[pltpu.roll(m[h][k], LANES - 1, 1) for k in range(3)] for h in range(2)]
         out = []
         for h in range(2):
@@ -313,27 +361,29 @@
 
 
 class Sums:
-    def __init__(self, init):
+    def __init__(self, init, squares=True):
         self.cross = list(init[0])
         self.square = list(init[1])
+        self.squares = squares
 
     def add(self, t, h, old, new):
         i = (2 * t + h) % len(self.cross)
         for k in range(3):
             self.cross[i] = self.cross[i] + old[k] * new[k]
-            self.square[i] = self.square[i] + new[k] * new[k]
+            if self.squares:
+                self.square[i] = self.square[i] + new[k] * new[k]
 
     def state(self):
         return (tuple(self.cross), tuple(self.square))
 
 
-def interior_kernel(m, es, w, v, tx_out, acc):
+def interior_kernel(m, es, w, v, tx_out, acc, squares=True):
     nl, tiles = m.shape[1], m.shape[2] // ROWS
     zero = jnp.zeros((ROWS, LANES), F32)
     tx_out[...] = jnp.zeros(tx_out.shape, F32)
 
     def layer(l, carry):
-        sums = Sums(carry)
+        sums = Sums(carry, squares)
         plane = Plane(
             lambda k, t, h: m[(k, l) + at(t, h)],
             lambda k, t, h: m[(k, l + 1) + at(t, h)],
@@ -354,11 +404,11 @@
     acc[1] = square[0] + square[1]
 
 
-def boundary_body(px, m, es, w, lo, hi, low_tensor, v_in, tx_in, acc_in, v, tx, acc):
+def boundary_body(m, es, w, lo, hi, low_tensor, v_in, tx_in, acc_in, v, tx, acc, squares=True):
     nl, tiles = m.shape[1], m.shape[2] // ROWS
     last = nl - 1
     zero = jnp.zeros((ROWS, LANES), F32)
-    sums = Sums(((zero, zero), (zero, zero)))
+    sums = Sums(((zero, zero), (zero, zero)), squares)
 
     below = Plane(lo, lambda k, t, h: m[(k, 0) + at(t, h)], low_tensor, tiles)
 
@@ -407,7 +457,7 @@
     even = (px == 0).astype(jnp.int32)
     nrow = xa.shape[1]
 
-    def unpack(a, b, rows, n):
+    def unpack(a, b, rows):
         def side(k, up):
             x, y = a(k), b(k)
             return choose(even, x, y) if up else choose(even, y, x)
@@ -421,10 +471,10 @@
 
     for t in range(nrow // 16):
         rows = pl.ds(16 * t, 16)
-        unpack(lambda k: xa[k, rows, :].astype(F32), lambda k: xb[k, rows, :].astype(F32), rows, 16)
-    unpack(lambda k: ca[k].astype(F32), lambda k: cb[k].astype(F32), pl.ds(nrow, ROWS), ROWS)
+        unpack(lambda k: xa[k, rows, :].astype(F32), lambda k: xb[k, rows, :].astype(F32), rows)
+    unpack(lambda k: ca[k].astype(F32), lambda k: cb[k].astype(F32), pl.ds(nrow, ROWS))
     boundary_body(
-        px, m, es, w,
+        m, es, w,
         lambda k, t, h: lo_s[(k,) + at(t, h)],
         lambda k, t, h: hi_s[(k,) + at(t, h)],
         lambda k, t, h: low[(k,) + at(t, h)],
@@ -433,12 +483,12 @@
     send_planes(px, v, ea, eb)
 
 
-def later_boundary(par, m, es, w, low, ra, rb, v_in, tx_in, acc_in, v, acc, tx):
+def later_boundary(par, m, es, w, low, ra, rb, v_in, tx_in, acc_in, v, acc, tx, squares=True):
     px = par[0]
     even = (px == 0).astype(jnp.int32)
     lo = lambda k, t, h: choose(even, rb[(k,) + at(t, h)], ra[(k,) + at(t, h)])
     hi = lambda k, t, h: choose(even, ra[(k,) + at(t, h)], rb[(k,) + at(t, h)])
-    boundary_body(px, m, es, w, lo, hi, lambda k, t, h: low[(k,) + at(t, h)], v_in, tx_in, acc_in, v, tx, acc)
+    boundary_body(m, es, w, lo, hi, lambda k, t, h: low[(k,) + at(t, h)], v_in, tx_in, acc_in, v, tx, acc, squares)
 
 
 def second_boundary_kernel(par, m, es, w, low, ra, rb, v_in, tx_in, acc_in, v, acc, ea, eb, tx):
@@ -449,7 +499,7 @@
 def third_boundary_kernel(
     par, m, es, w, low, ra, rb, v_in, tx_in, acc_in, acc0, acc1, acc2, v, parts, tx, acc
 ):
-    later_boundary(par, m, es, w, low, ra, rb, v_in, tx_in, acc_in, v, acc, tx)
+    later_boundary(par, m, es, w, low, ra, rb, v_in, tx_in, acc_in, v, acc, tx, False)
     _, lane = iotas()
     line = jnp.zeros((ROWS, LANES), F32)
     terms = [acc0[0], acc0[1], acc1[0], acc1[1], acc2[0], acc2[1], acc[0]]
@@ -507,41 +557,37 @@
         for i in range(7)
     ]
     held = term[1]
-    moment = [term[0] + held] + [term[i] + held for i in range(2, 7)]
+    moment = [term[0]] + [term[i] + held for i in range(2, 7)]
     c = coefficients(moment)
     both = c[0] + c[1] + c[2]
+    rest = 1.0 - both
+
+    def copies(l):
+        return [
+            pltpu.make_async_copy(xs.at[l], x.at[:, l], sem.at[l, 0]),
+            pltpu.make_async_copy(rs.at[l], r.at[:, l], sem.at[l, 1]),
+        ]
+
+    def layer(l, _):
+        for t in range(nrow // ROWS):
+            for h in range(2):
+                rows, cols = at(t, h)
+                free = w[l, rows, cols] > 0.0
+                fx = jnp.where(free, c[0], both)
+                fr = jnp.where(free, 1.0, rest)
+                for k in range(3):
+                    b = raw[k, l, rows, cols]
+                    v1, v2, v3 = m1[k, l, rows, cols], m2[k, l, rows, cols], m3[k, l, rows, cols]
+                    xs[l, k, rows, cols] = fx * b + (c[1] * v1 + c[2] * v2)
+                    rs[l, k, rows, cols] = fr * b - (c[0] * v1 + c[1] * v2 + c[2] * v3)
+        for copy in copies(l):
+            copy.start()
+        return 0
+
+    lax.fori_loop(0, nl, layer, 0)
     for l in range(nl):
-        slot = l % 2
-        copies = [
-            pltpu.make_async_copy(xs.at[slot], x.at[:, l], sem.at[slot, 0]),
-            pltpu.make_async_copy(rs.at[slot], r.at[:, l], sem.at[slot, 1]),
-        ]
-        if l >= 2:
-            for copy in copies:
-                copy.wait()
-
-        def chunk(u, _):
-            for i in range(4):
-                for h in range(2):
-                    rows = pl.ds(pl.multiple_of(ROWS * (4 * u + i), ROWS), ROWS)
-                    cols = pl.ds(LANES * h, LANES)
-                    free = w[l, rows, cols] > 0.0
-                    fx = jnp.where(free, c[0], both)
-                    fr = jnp.where(free, 1.0, 1.0 - both)
-                    for k in range(3):
-                        b = raw[k, l, rows, cols]
-                        v1, v2, v3 = m1[k, l, rows, cols], m2[k, l, rows, cols], m3[k, l, rows, cols]
-                        xs[slot, k, rows, cols] = fx * b + (c[1] * v1 + c[2] * v2)
-                        rs[slot, k, rows, cols] = fr * b - (c[0] * v1 + c[1] * v2 + c[2] * v3)
-            return 0
-
-        lax.fori_loop(0, nrow // (4 * ROWS), chunk, 0)
-        for copy in copies:
-            copy.start()
-    for l in range(max(0, nl - 2), nl):
-        slot = l % 2
-        pltpu.make_async_copy(xs.at[slot], x.at[:, l], sem.at[slot, 0]).wait()
-        pltpu.make_async_copy(rs.at[slot], r.at[:, l], sem.at[slot, 1]).wait()
+        for copy in copies(l):
+            copy.wait()
 
 
 def exchange(x, axis, first):
@@ -552,30 +598,34 @@
     return lax.ppermute(x, axis, pairs)
 
 
-def per_device(b, visc, strain, code):
+def device_program(b, visc, strain, code):
     _, nl, nrow, nz = b.shape
     rows = nrow + ROWS
     par = jnp.stack([lax.axis_index("gx") % 2, lax.axis_index("yz") % 2]).astype(jnp.int32)
     peers = lax.axis_size("gx") * lax.axis_size("yz")
     S = jax.ShapeDtypeStruct
 
-    ya, yb, xa, xb = call(
-        pack_kernel, "pack",
-        [("smem", par), ("hbm", b), ("hbm", visc), ("hbm", strain), ("hbm", code)],
-        [resident((14, nl, ROWS, nz), BF16)] * 2 + [resident((13, nrow, nz), BF16)] * 2,
+    inputs = [("hbm", b), ("hbm", visc), ("hbm", strain), ("hbm", code)]
+    ya, yb, token = call(
+        pack_y_kernel, [("smem", par)] + inputs,
+        [resident((nl, 48, nz), BF16)] * 2 + [resident((ROWS, LANES))],
         scratch=[
             VMEM((2, 3, nl, ROWS, nz), F32), VMEM((2, nl, ROWS, nz), BF16), VMEM((2, 6, nl, ROWS, nz), BF16),
-            VMEM((2, nl, ROWS, nz), jnp.int32), VMEM((2, 3, nrow, nz), F32), VMEM((2, nrow, nz), jnp.int32),
-            pltpu.SemaphoreType.DMA((2, 8)),
+            VMEM((2, nl, ROWS, nz), jnp.int32), pltpu.SemaphoreType.DMA((2, 4)),
         ],
         cost=(1e6, 2e6),
     )
     rya, ryb = exchange(ya, "yz", 0), exchange(yb, "yz", 1)
+    xa, xb = call(
+        pack_x_kernel, [("smem", par)] + inputs + [("v", token)],
+        [resident((13, nrow, nz), BF16)] * 2,
+        scratch=[VMEM((2, 3, nrow, nz), F32), VMEM((2, nrow, nz), jnp.int32), pltpu.SemaphoreType.DMA((2, 8))],
+        cost=(1e6, 2e6),
+    )
     rxa, rxb = exchange(xa, "gx", 0), exchange(xb, "gx", 1)
 
     raw, es, m0, w, acc0 = call(
-        load_kernel, "load",
-        [("hbm", b), ("hbm", visc), ("hbm", strain), ("hbm", code)],
+        load_kernel, inputs,
         [
             resident((3, nl, nrow, nz)), resident((nl, 7, rows, nz)), resident((3, nl, rows, nz)),
             resident((nl, rows, nz)), resident((2, ROWS, LANES)),
@@ -587,7 +637,7 @@
         cost=(2e7, 9e6),
     )
     es, m0, w, ca, cb = call(
-        halo_kernel, "halo",
+        halo_kernel,
         [("smem", par), ("v", rya), ("v", ryb), ("v", es), ("v", m0), ("v", w)],
         [
             resident((nl, 7, rows, nz)), resident((3, nl, rows, nz)), resident((nl, rows, nz)),
@@ -603,11 +653,9 @@
     tx_scratch = VMEM((3, rows, nz), F32)
     work = (4e7, 1e7)
 
-    v, tx, acc = call(
-        interior_kernel, "interior1", [("v", m0), ("v", es), ("v", w)], [field, plane, sums], cost=work
-    )
+    v, tx, acc = call(interior_kernel, [("v", m0), ("v", es), ("v", w)], [field, plane, sums], cost=work)
     m1, acc1, low, ea, eb = call(
-        first_boundary_kernel, "boundary1",
+        first_boundary_kernel,
         [("smem", par), ("v", m0), ("v", es), ("v", w), ("v", rxa), ("v", rxb), ("v", rca), ("v", rcb),
          ("v", v), ("v", tx), ("v", acc)],
         [field, sums, resident((7, rows, nz)), plane, plane],
@@ -615,11 +663,9 @@
         aliases={8: 0},
     )
     ra, rb = exchange(ea, "gx", 0), exchange(eb, "gx", 1)
-    v, tx, acc = call(
-        interior_kernel, "interior2", [("v", m1), ("v", es), ("v", w)], [field, plane, sums], cost=work
-    )
+    v, tx, acc = call(interior_kernel, [("v", m1), ("v", es), ("v", w)], [field, plane, sums], cost=work)
     m2, acc2, ea, eb = call(
-        second_boundary_kernel, "boundary2",
+        second_boundary_kernel,
         [("smem", par), ("v", m1), ("v", es), ("v", w), ("v", low), ("v", ra), ("v", rb),
          ("v", v), ("v", tx), ("v", acc)],
         [field, sums, plane, plane],
@@ -628,10 +674,10 @@
     )
     ra, rb = exchange(ea, "gx", 0), exchange(eb, "gx", 1)
     v, tx, acc = call(
-        interior_kernel, "interior3", [("v", m2), ("v", es), ("v", w)], [field, plane, sums], cost=work
+        functools.partial(interior_kernel, squares=False), [("v", m2), ("v", es), ("v", w)], [field, plane, sums], cost=work
     )
     m3, parts = call(
-        third_boundary_kernel, "boundary3",
+        third_boundary_kernel,
         [("smem", par), ("v", m2), ("v", es), ("v", w), ("v", low), ("v", ra), ("v", rb),
          ("v", v), ("v", tx), ("v", acc), ("v", acc0), ("v", acc1), ("v", acc2)],
         [field, resident((peers, LANES))],
@@ -640,10 +686,10 @@
     )
     gathered = lax.all_to_all(parts, ("gx", "yz"), 0, 0)
     return call(
-        output_kernel, "output",
+        output_kernel,
         [("v", gathered), ("v", raw), ("v", w), ("v", m1), ("v", m2), ("v", m3)],
         [S(b.shape, F32), S(b.shape, F32)],
-        scratch=[VMEM((2, 3, nrow, nz), F32), VMEM((2, 3, nrow, nz), F32), pltpu.SemaphoreType.DMA((2, 2))],
+        scratch=[VMEM((nl, 3, nrow, nz), F32), VMEM((nl, 3, nrow, nz), F32), pltpu.SemaphoreType.DMA((nl, 2))],
     )
 
 
@@ -655,7 +701,7 @@
         P("gx", "yz", None),
     )
     return jax.shard_map(
-        per_device,
+        device_program,
         mesh=mesh,
         in_specs=placed,
         out_specs=(P(None, "gx", "yz", None), P(None, "gx", "yz", None)),

time: 89.1 us -> 78.4 us (0.88)
  local copies, waits for them, and re-layouts: 6.05 us -> 0 us
  starting transfers between devices: 20.1 us -> 18.3 us
  waiting for transfers between devices: 3.66 us -> 2.16 us
  Pallas kernels: 34.3 us -> 33.1 us
    unnamed x14 -> x0, local copies, waits for them, and re-layouts: 6.05 us -> none
    ppermute x10, starting transfers between devices: 20.1 us -> 18.3 us  [exchange(): return lax.ppermute(x, axis, pairs)]
    ppermute x10, waiting for transfers between devices: 3.66 us -> 2.16 us  [exchange(): return lax.ppermute(x, axis, pairs)]
    pallas_call x10 -> x11, Pallas kernels: 34.3 us -> 33.1 us  [call(): pl.pallas_call(kernel, out_shape=outs, in_specs=specs, out_specs=out_spec...]
  transfers between devices with their start and end apart: 10 -> 10, of which waited for: 3 -> 2; matrix products, arithmetic and copies ran while one was open for 0% -> 0% of each run, Pallas kernels for 24% -> 25%
where the time goes in v2:
time: 78.4 us; the launch traced here: 78.1 us
  Pallas kernels  33.1 us (42%)
  blocking collectives  23.5 us (30%)
  starting transfers between devices  18.3 us (23%)
  waiting for transfers between devices  2.16 us (3%)
  between operations  0.84 us (1%)
    pallas_call x11, Pallas kernels, call(): pl.pallas_call(kernel, out_shape=outs, in_specs=specs, out_specs=out_spec...  33.1 us
    all_to_all x1, blocking collectives, device_program(): gathered = lax.all_to_all(parts, ('gx', 'yz'), 0, 0)  23.5 us
    ppermute x10, starting transfers between devices, exchange(): return lax.ppermute(x, axis, pairs)  18.3 us
    ppermute x10, waiting for transfers between devices, exchange(): return lax.ppermute(x, axis, pairs)  2.16 us
  transfers between devices with their start and end apart: 10, of which 2 were waited for; matrix products, arithmetic and copies ran while one was open for 0% of the time, Pallas kernels for 25%

profile of v2, /device:TPU:1, one launch (start us, length us, event | category | flops | bytes accessed | tf_op | source)
XLA Modules:
  0.0 78.1 jit_solution(10505607984658211757)
XLA Ops:
  0.7 2.3 %shard_map.59 = (bf16[8,48,256]{2,1,0:T(8,128)(2,1)S(1)}, bf16[8,48,256]{2,1,0:T(8,128)(2,1)S(1)}, f32[8,128]{1,0:T(8,128)S(1)}) custom-call(s32[2]{0:T(128)S(1)} %pad_add_fusion.par, f32[3,8,128,256]{3,2,1,0:T(8,128)} %b.5, bf16[8,128,256]{2,1,0:T(8,128)(2,1)} %visc.5, bf16[6,8,128,256]{3,2,1,0:T(8,128)(2,1)} %strain.5, s32[8,128,256]{2,1,0:T(8,128)} %code.5), custom_call_target="tpu_custom_call" | custom-call | flops 1000000 | bytes 2000000 | tf_op jit(solution)/shard_map/pallas_call | solution.py:44
  3.0 2.2 %shard_map.62 = (bf16[13,128,256]{2,1,0:T(8,128)(2,1)S(1)}, bf16[13,128,256]{2,1,0:T(8,128)(2,1)S(1)}) custom-call(s32[2]{0:T(128)S(1)} %pad_add_fusion.par, f32[3,8,128,256]{3,2,1,0:T(8,128)} %b.5, bf16[8,128,256]{2,1,0:T(8,128)(2,1)} %visc.5, bf16[6,8,128,256]{3,2,1,0:T(8,128)(2,1)} %strain.5, s32[8,128,256]{2,1,0:T(8,128)} %code.5, ...), custom_call_target="tpu_custom_call" | custom-call | flops 1000000 | bytes 2000000 | tf_op jit(solution)/shard_map/pallas_call | solution.py:44
  5.2 1.5 %collective-permute-start.2 = (bf16[13,128,256]{2,1,0:T(8,128)(2,1)S(1)}, bf16[13,128,256]{2,1,0:T(8,128)(2,1)S(1)}, u32[]{:S(2)}, u32[]{:S(2)}) collective-permute-start(bf16[13,128,256]{2,1,0:T(8,128)(2,1)S(1)} %get-tuple-element.46), channel_id=1, source_target_pairs={{0,16},{16,0},{32,48},{48,32},{64,80},{80,64},{96,112},{112,96},{1... | collective-permute-start | bytes 2555912 | tf_op jit(solution)/shard_map/ppermute | solution.py:598
  6.7 3.1 %collective-permute-start.3 = (bf16[13,128,256]{2,1,0:T(8,128)(2,1)S(1)}, bf16[13,128,256]{2,1,0:T(8,128)(2,1)S(1)}, u32[]{:S(2)}, u32[]{:S(2)}) collective-permute-start(bf16[13,128,256]{2,1,0:T(8,128)(2,1)S(1)} %get-tuple-element.47), channel_id=1, source_target_pairs={{16,32},{32,16},{48,64},{64,48},{80,96},{96,80},{17,33},{33,17},{4... | collective-permute-start | bytes 2555912 | tf_op jit(solution)/shard_map/ppermute | solution.py:598
  9.8 1.7 %collective-permute-start = (bf16[8,48,256]{2,1,0:T(8,128)(2,1)S(1)}, bf16[8,48,256]{2,1,0:T(8,128)(2,1)S(1)}, u32[]{:S(2)}, u32[]{:S(2)}) collective-permute-start(bf16[8,48,256]{2,1,0:T(8,128)(2,1)S(1)} %get-tuple-element.37), channel_id=1, source_target_pairs={{0,1},{1,0},{2,3},{3,2},{4,5},{5,4},{6,7},{7,6},{8,9},{9,8},{10,11... | collective-permute-start | bytes 589832 | tf_op jit(solution)/shard_map/ppermute | solution.py:598
  11.6 0.7 collective-permute-start.1
  12.2 3.7 %shard_map.60 = (f32[3,8,128,256]{3,2,1,0:T(8,128)S(1)}, f32[8,7,136,256]{3,2,1,0:T(8,128)S(1)}, f32[3,8,136,256]{3,2,1,0:T(8,128)S(1)}, f32[8,136,256]{2,1,0:T(8,128)S(1)}, f32[2,8,128]{2,1,0:T(8,128)S(1)}) custom-call(f32[3,8,128,256]{3,2,1,0:T(8,128)} %b.5, bf16[8,128,256]{2,1,0:T(8,128)(2,1)} %visc.5, bf16[6,8,128,256]{3,2,1,0:T(8,128)(2,1)} %strain.5, ...), custom_call_target="tpu_custom_call" | custom-call | flops 20000000 | bytes 9000000 | tf_op jit(solution)/shard_map/pallas_call | solution.py:44
  16.0 1.0 %shard_map.61 = (f32[8,7,136,256]{3,2,1,0:T(8,128)S(1)}, f32[3,8,136,256]{3,2,1,0:T(8,128)S(1)}, f32[8,136,256]{2,1,0:T(8,128)S(1)}, bf16[13,8,256]{2,1,0:T(8,128)(2,1)S(1)}, bf16[13,8,256]{2,1,0:T(8,128)(2,1)S(1)}) custom-call(s32[2]{0:T(128)S(1)} %pad_add_fusion.par, ...), custom_call_target="tpu_custom_call", output_to_operand_aliasing={{0}: (3, {}), {1}: (4, {}), {2}: (5, {})} | custom-call | flops 1000000 | bytes 1000000 | tf_op jit(solution)/shard_map/pallas_call | solution.py:44
  17.0 0.1 collective-permute-start.4
  17.1 4.2 %collective-permute-start.5 = (bf16[13,8,256]{2,1,0:T(8,128)(2,1)S(1)}, bf16[13,8,256]{2,1,0:T(8,128)(2,1)S(1)}, u32[]{:S(2)}, u32[]{:S(2)}) collective-permute-start(bf16[13,8,256]{2,1,0:T(8,128)(2,1)S(1)} %get-tuple-element.49), channel_id=1, source_target_pairs={{16,32},{32,16},{48,64},{64,48},{80,96},{96,80},{17,33},{33,17},{4... | collective-permute-start | bytes 159752 | tf_op jit(solution)/shard_map/ppermute | solution.py:598
  21.3 5.0 %shard_map.63 = (f32[3,8,136,256]{3,2,1,0:T(8,128)S(1)}, f32[3,136,256]{2,1,0:T(8,128)S(1)}, f32[2,8,128]{2,1,0:T(8,128)S(1)}) custom-call(f32[3,8,136,256]{3,2,1,0:T(8,128)S(1)} %get-tuple-element.42.m, f32[8,7,136,256]{3,2,1,0:T(8,128)S(1)} %get-tuple-element.43.es, f32[8,136,256]{2,1,0:T(8,128)S(1)} %get-tuple-element.44.w), custom_call_target="tpu_custom_call" | custom-call | flops 40000000 | bytes 10000000 | tf_op jit(solution)/shard_map/pallas_call | solution.py:44
  26.4 2.3 %shard_map.64 = (f32[3,8,136,256]{3,2,1,0:T(8,128)S(1)}, f32[2,8,128]{2,1,0:T(8,128)S(1)}, f32[7,136,256]{2,1,0:T(8,128)S(1)}, f32[3,136,256]{2,1,0:T(8,128)S(1)}, f32[3,136,256]{2,1,0:T(8,128)S(1)}) custom-call(s32[2]{0:T(128)S(1)} %pad_add_fusion.par, f32[3,8,136,256]{3,2,1,0:T(8,128)S(1)} %get-tuple-element.42.m, ...), custom_call_target="tpu_custom_call", output_to_operand_aliasing={{0}: (8, {})} | custom-call | flops 1000000 | bytes 1000000 | tf_op jit(solution)/shard_map/pallas_call | solution.py:44
  28.7 0.1 collective-permute-start.6
  28.8 3.4 %collective-permute-start.7 = (f32[3,136,256]{2,1,0:T(8,128)S(1)}, f32[3,136,256]{2,1,0:T(8,128)S(1)}, u32[]{:S(2)}, u32[]{:S(2)}) collective-permute-start(f32[3,136,256]{2,1,0:T(8,128)S(1)} %get-tuple-element.56), channel_id=1, source_target_pairs={{16,32},{32,16},{48,64},{64,48},{80,96},{96,80},{17,33},{33,17},{4... | collective-permute-start | bytes 1253384 | tf_op jit(solution)/shard_map/ppermute | solution.py:598
  32.2 4.9 %shard_map.65 = (f32[3,8,136,256]{3,2,1,0:T(8,128)S(1)}, f32[3,136,256]{2,1,0:T(8,128)S(1)}, f32[2,8,128]{2,1,0:T(8,128)S(1)}) custom-call(f32[3,8,136,256]{3,2,1,0:T(8,128)S(1)} %get-tuple-element.53.m.m1, f32[8,7,136,256]{3,2,1,0:T(8,128)S(1)} %get-tuple-element.43.es, f32[8,136,256]{2,1,0:T(8,128)S(1)} %get-tuple-element.44.w), custom_call_target="tpu_custom_call" | custom-call | flops 40000000 | bytes 10000000 | tf_op jit(solution)/shard_map/pallas_call | solution.py:44
  37.1 1.0 %collective-permute-done.7.rb = f32[3,136,256]{2,1,0:T(8,128)S(1)} collective-permute-done((f32[3,136,256]{2,1,0:T(8,128)S(1)}, f32[3,136,256]{2,1,0:T(8,128)S(1)}, u32[]{:S(2)}, u32[]{:S(2)}) %collective-permute-start.7) | collective-permute-done | bytes 417824 | tf_op jit(solution)/shard_map/ppermute | solution.py:598
  38.2 2.1 %shard_map.66 = (f32[3,8,136,256]{3,2,1,0:T(8,128)S(1)}, f32[2,8,128]{2,1,0:T(8,128)S(1)}, f32[3,136,256]{2,1,0:T(8,128)S(1)}, f32[3,136,256]{2,1,0:T(8,128)S(1)}) custom-call(s32[2]{0:T(128)S(1)} %pad_add_fusion.par, f32[3,8,136,256]{3,2,1,0:T(8,128)S(1)} %get-tuple-element.53.m.m1, ...), custom_call_target="tpu_custom_call", output_to_operand_aliasing={{0}: (7, {})} | custom-call | flops 1000000 | bytes 1000000 | tf_op jit(solution)/shard_map/pallas_call | solution.py:44
  40.2 0.1 collective-permute-start.8
  40.3 3.5 %collective-permute-start.9 = (f32[3,136,256]{2,1,0:T(8,128)S(1)}, f32[3,136,256]{2,1,0:T(8,128)S(1)}, u32[]{:S(2)}, u32[]{:S(2)}) collective-permute-start(f32[3,136,256]{2,1,0:T(8,128)S(1)} %get-tuple-element.62), channel_id=1, source_target_pairs={{16,32},{32,16},{48,64},{64,48},{80,96},{96,80},{17,33},{33,17},{4... | collective-permute-start | bytes 1253384 | tf_op jit(solution)/shard_map/ppermute | solution.py:598
  43.8 4.7 %shard_map.67 = (f32[3,8,136,256]{3,2,1,0:T(8,128)S(1)}, f32[3,136,256]{2,1,0:T(8,128)S(1)}, f32[2,8,128]{2,1,0:T(8,128)S(1)}) custom-call(f32[3,8,136,256]{3,2,1,0:T(8,128)S(1)} %get-tuple-element.60.m.m2, f32[8,7,136,256]{3,2,1,0:T(8,128)S(1)} %get-tuple-element.43.es, f32[8,136,256]{2,1,0:T(8,128)S(1)} %get-tuple-element.44.w), custom_call_target="tpu_custom_call" | custom-call | flops 40000000 | bytes 10000000 | tf_op jit(solution)/shard_map/pallas_call | solution.py:44
  48.6 1.1 %collective-permute-done.9.rb = f32[3,136,256]{2,1,0:T(8,128)S(1)} collective-permute-done((f32[3,136,256]{2,1,0:T(8,128)S(1)}, f32[3,136,256]{2,1,0:T(8,128)S(1)}, u32[]{:S(2)}, u32[]{:S(2)}) %collective-permute-start.9) | collective-permute-done | bytes 417824 | tf_op jit(solution)/shard_map/ppermute | solution.py:598
  49.7 1.8 %shard_map.68 = (f32[3,8,136,256]{3,2,1,0:T(8,128)S(1)}, f32[128,128]{1,0:T(8,128)S(1)}) custom-call(s32[2]{0:T(128)S(1)} %pad_add_fusion.par, f32[3,8,136,256]{3,2,1,0:T(8,128)S(1)} %get-tuple-element.60.m.m2, f32[8,7,136,256]{3,2,1,0:T(8,128)S(1)} %get-tuple-element.43.es, ...), custom_call_target="tpu_custom_call", output_to_operand_aliasing={{0}: (7, {})} | custom-call | flops 1000000 | bytes 1000000 | tf_op jit(solution)/shard_map/pallas_call | solution.py:44
  51.5 23.5 %all_to_all.11 = f32[128,1,128]{2,1,0:T(1,128)S(1)} all-to-all(f32[128,1,128]{2,1,0:T(1,128)S(1)} %bitcast.7), channel_id=1, replica_groups=mesh['gx'=8,'yz'=16] {'gx','yz'}, dimensions={0} | all-to-all | bytes 131072 | tf_op jit(solution)/shard_map/all_to_all | solution.py:687
  75.0 3.1 %shard_map.69 = (f32[3,8,128,256]{3,2,1,0:T(8,128)}, f32[3,8,128,256]{3,2,1,0:T(8,128)}) custom-call(f32[128,128]{1,0:T(8,128)S(1)} %bitcast.6, f32[3,8,128,256]{3,2,1,0:T(8,128)S(1)} %get-tuple-element.70.raw, f32[8,136,256]{2,1,0:T(8,128)S(1)} %get-tuple-element.44.w, f32[3,8,136,256]{3,2,1,0:T(8,128)S(1)} %get-tuple-element.53.m.m1, ...), custom_call_target="tpu_custom_call" | custom-call | flops 1000000 | bytes 1000000 | tf_op jit(solution)/shard_map/pallas_call | solution.py:44
  (9 shorter events, 0.1 us)
Async XLA Ops:
  5.2 21.1 %collective-permute-start.2 = (bf16[13,128,256]{2,1,0:T(8,128)(2,1)S(1)}, bf16[13,128,256]{2,1,0:T(8,128)(2,1)S(1)}, u32[]{:S(2)}, u32[]{:S(2)}) collective-permute-start(bf16[13,128,256]{2,1,0:T(8,128)(2,1)S(1)} %get-tuple-element.46), channel_id=1, source_target_pairs={{0,16},{16,0},{32,48},{48,32},{64,80},{80,64},{96,112},{112,96},{1... | collective-permute-start | bytes 2555912 | tf_op jit(solution)/shard_map/ppermute | solution.py:598
  6.7 19.7 %collective-permute-start.3 = (bf16[13,128,256]{2,1,0:T(8,128)(2,1)S(1)}, bf16[13,128,256]{2,1,0:T(8,128)(2,1)S(1)}, u32[]{:S(2)}, u32[]{:S(2)}) collective-permute-start(bf16[13,128,256]{2,1,0:T(8,128)(2,1)S(1)} %get-tuple-element.47), channel_id=1, source_target_pairs={{16,32},{32,16},{48,64},{64,48},{80,96},{96,80},{17,33},{33,17},{4... | collective-permute-start | bytes 2555912 | tf_op jit(solution)/shard_map/ppermute | solution.py:598
  9.8 6.1 %collective-permute-start = (bf16[8,48,256]{2,1,0:T(8,128)(2,1)S(1)}, bf16[8,48,256]{2,1,0:T(8,128)(2,1)S(1)}, u32[]{:S(2)}, u32[]{:S(2)}) collective-permute-start(bf16[8,48,256]{2,1,0:T(8,128)(2,1)S(1)} %get-tuple-element.37), channel_id=1, source_target_pairs={{0,1},{1,0},{2,3},{3,2},{4,5},{5,4},{6,7},{7,6},{8,9},{9,8},{10,11... | collective-permute-start | bytes 589832 | tf_op jit(solution)/shard_map/ppermute | solution.py:598
  11.6 4.4 %collective-permute-start.1 = (bf16[8,48,256]{2,1,0:T(8,128)(2,1)S(1)}, bf16[8,48,256]{2,1,0:T(8,128)(2,1)S(1)}, u32[]{:S(2)}, u32[]{:S(2)}) collective-permute-start(bf16[8,48,256]{2,1,0:T(8,128)(2,1)S(1)} %get-tuple-element.38), channel_id=1, source_target_pairs={{1,2},{2,1},{3,4},{4,3},{5,6},{6,5},{7,8},{8,7},{9,10},{10,9},{11,... | collective-permute-start | bytes 589832 | tf_op jit(solution)/shard_map/ppermute | solution.py:598
  17.0 9.3 %collective-permute-start.4 = (bf16[13,8,256]{2,1,0:T(8,128)(2,1)S(1)}, bf16[13,8,256]{2,1,0:T(8,128)(2,1)S(1)}, u32[]{:S(2)}, u32[]{:S(2)}) collective-permute-start(bf16[13,8,256]{2,1,0:T(8,128)(2,1)S(1)} %get-tuple-element.48), channel_id=1, source_target_pairs={{0,16},{16,0},{32,48},{48,32},{64,80},{80,64},{96,112},{112,96},{1... | collective-permute-start | bytes 159752 | tf_op jit(solution)/shard_map/ppermute | solution.py:598
  17.1 9.2 %collective-permute-start.5 = (bf16[13,8,256]{2,1,0:T(8,128)(2,1)S(1)}, bf16[13,8,256]{2,1,0:T(8,128)(2,1)S(1)}, u32[]{:S(2)}, u32[]{:S(2)}) collective-permute-start(bf16[13,8,256]{2,1,0:T(8,128)(2,1)S(1)} %get-tuple-element.49), channel_id=1, source_target_pairs={{16,32},{32,16},{48,64},{64,48},{80,96},{96,80},{17,33},{33,17},{4... | collective-permute-start | bytes 159752 | tf_op jit(solution)/shard_map/ppermute | solution.py:598
  28.7 8.4 %collective-permute-start.6 = (f32[3,136,256]{2,1,0:T(8,128)S(1)}, f32[3,136,256]{2,1,0:T(8,128)S(1)}, u32[]{:S(2)}, u32[]{:S(2)}) collective-permute-start(f32[3,136,256]{2,1,0:T(8,128)S(1)} %get-tuple-element.55), channel_id=1, source_target_pairs={{0,16},{16,0},{32,48},{48,32},{64,80},{80,64},{96,112},{112,96},{1... | collective-permute-start | bytes 1253384 | tf_op jit(solution)/shard_map/ppermute | solution.py:598
  28.8 9.4 %collective-permute-start.7 = (f32[3,136,256]{2,1,0:T(8,128)S(1)}, f32[3,136,256]{2,1,0:T(8,128)S(1)}, u32[]{:S(2)}, u32[]{:S(2)}) collective-permute-start(f32[3,136,256]{2,1,0:T(8,128)S(1)} %get-tuple-element.56), channel_id=1, source_target_pairs={{16,32},{32,16},{48,64},{64,48},{80,96},{96,80},{17,33},{33,17},{4... | collective-permute-start | bytes 1253384 | tf_op jit(solution)/shard_map/ppermute | solution.py:598
  40.2 8.3 %collective-permute-start.8 = (f32[3,136,256]{2,1,0:T(8,128)S(1)}, f32[3,136,256]{2,1,0:T(8,128)S(1)}, u32[]{:S(2)}, u32[]{:S(2)}) collective-permute-start(f32[3,136,256]{2,1,0:T(8,128)S(1)} %get-tuple-element.61), channel_id=1, source_target_pairs={{0,16},{16,0},{32,48},{48,32},{64,80},{80,64},{96,112},{112,96},{1... | collective-permute-start | bytes 1253384 | tf_op jit(solution)/shard_map/ppermute | solution.py:598
  40.3 9.4 %collective-permute-start.9 = (f32[3,136,256]{2,1,0:T(8,128)S(1)}, f32[3,136,256]{2,1,0:T(8,128)S(1)}, u32[]{:S(2)}, u32[]{:S(2)}) collective-permute-start(f32[3,136,256]{2,1,0:T(8,128)S(1)} %get-tuple-element.62), channel_id=1, source_target_pairs={{16,32},{32,16},{48,64},{64,48},{80,96},{96,80},{17,33},{33,17},{4... | collective-permute-start | bytes 1253384 | tf_op jit(solution)/shard_map/ppermute | solution.py:598
